TPU v7x, 32 devices: a whole 2x2x4 slice. The times are simulated.
32 devices in a mesh: fsdp: 8 (over y, x, core), tp: 4 (over z).
Axes of the slice: x: 2, y: 2, z: 4, core: 2. Of those that a mesh axis runs over, the one named last changes fastest.
Arguments:
- residual: bfloat16 [4096, 2048], P(('fsdp', 'tp')), may hold values from -6 to 6
- norm_gain: bfloat16 [2048], P(('fsdp', 'tp')), may hold values from 0.099609375 to 1.8984375
- norm_shift: bfloat16 [2048], P(('fsdp', 'tp')), may hold values from -1.75 to 1.75
- qkv_weight: bfloat16 [3, 2048, 2048], P(None, 'fsdp', 'tp'), may hold values from -0.125 to 0.125
- qkv_bias: bfloat16 [3, 2048], P(None, ('tp', 'fsdp')), may hold values from -1.75 to 1.75
- dense_weight: bfloat16 [2048, 2048], P('tp', 'fsdp'), may hold values from -0.75 to 0.75
- dense_bias: bfloat16 [2048], P(('fsdp', 'tp')), may hold values from -1.75 to 1.75
- inner_weight: bfloat16 [2048, 8192], P('fsdp', 'tp'), may hold values from -0.125 to 0.125
- inner_bias: bfloat16 [8192], P(('tp', 'fsdp')), may hold values from -1.75 to 1.75
- outer_weight: bfloat16 [8192, 2048], P('tp', 'fsdp'), may hold values from -0.0625 to 0.0625
- outer_bias: bfloat16 [2048], P(('fsdp', 'tp')), may hold values from -1.75 to 1.75
- cotangent: bfloat16 [4096, 2048], P(('fsdp', 'tp')), may hold values from -6 to 6
- segment: int32 [4096], replicated, may hold values from 0 to 38, as said below
- ancestors: int32 [39, 3], replicated, may hold values from 0 to 38, as said below
- valid_slot: int32 [4096], replicated, may hold values from 0 to 1, as said below
Outputs:
- output: bfloat16 [4096, 2048], P(('fsdp', 'tp'))
- residual_grad: bfloat16 [4096, 2048], P(('fsdp', 'tp'))
- norm_gain_grad: float32 [2048], P(('fsdp', 'tp'))
- norm_shift_grad: float32 [2048], P(('fsdp', 'tp'))
- qkv_weight_grad: float32 [3, 2048, 2048], P(None, 'fsdp', 'tp')
- qkv_bias_grad: float32 [3, 2048], P(None, ('tp', 'fsdp'))
- dense_weight_grad: float32 [2048, 2048], P('tp', 'fsdp')
- dense_bias_grad: float32 [2048], P(('fsdp', 'tp'))
- inner_weight_grad: float32 [2048, 8192], P('fsdp', 'tp')
- inner_bias_grad: float32 [8192], P(('tp', 'fsdp'))
- outer_weight_grad: float32 [8192, 2048], P('tp', 'fsdp')
- outer_bias_grad: float32 [2048], P(('fsdp', 'tp'))
Inputs may be any that keep to these rules, and one draw needn't show every extreme that they name: Each of the 3 trees fills 1024 consecutive slots, in order of slots: a trunk of 640 slots, then four branches and eight leaves of 32 slots each, two leaves to a branch, each leaf after its branch; the slots of a segment are consecutive and carry its id; padding slots carry 0. `ancestors`: row s names the trunk, branch and leaf segment of the path that ends in segment s, repeating s where the path is shorter; each tree's segments name only that tree's segments. `valid_slot`: 1 on exactly the slots that trees fill, 0 on the other 1024 slots.
All inputs are finite; a program needn't handle non-finite values.
Results may differ from a plain program's by a relative error of at most 0.0098.
Values may be sent and summed in bfloat16 or wider, within the bound.
No kernel may reach another device: no remote copies, remote signals or barrier semaphores. Data moves between devices by JAX's collectives and lax.ppermute only.
A program may use at most 192 MiB of HBM per device.

v0:
```python
import jax
import jax.numpy as jnp
from jax import lax
from jax.sharding import PartitionSpec as P

HEAD_DIM = 64
ROTARY = 32
TREE_LEN = 1024


EPSILON = 1e-05


def passed_along(value, axis, steps):
    count = lax.axis_size(axis)
    initial, last = (max(0, -steps), min(count, count - steps))
    return lax.ppermute(value, axis, [(source, source + steps) for source in range(initial, last)])


def norm_rows(inputs_f, gain_f, shift_f):
    row_mean = jnp.mean(inputs_f, axis=-1, keepdims=True)
    centered = inputs_f - row_mean
    variance = jnp.mean(centered * centered, axis=-1, keepdims=True)
    return centered * lax.rsqrt(variance + EPSILON) * gain_f + shift_f


def tree_allowed(query_seg, query_slot, query_valid, key_seg, key_slot, key_valid, ancestors):
    seg_ids = jnp.arange(ancestors.shape[0], dtype=jnp.int32)
    onehot = (query_seg[:, None] == seg_ids[None, :]).astype(jnp.int32)
    path_ids = jnp.sum(onehot[:, :, None] * ancestors[None, :, :], axis=1)
    linked = (
        (key_seg[None, :] == path_ids[:, 0:1])
        | (key_seg[None, :] == path_ids[:, 1:2])
        | (key_seg[None, :] == path_ids[:, 2:3])
    )
    earlier = key_slot[None, :] <= query_slot[:, None]
    usable = (key_valid[None, :] == 1) & (query_valid[:, None] == 1)
    return linked & earlier & usable | (key_slot[None, :] == query_slot[:, None])


def rotate(tensor, positions, direction):
    half_rot = ROTARY // 2
    freq = 10000.0 ** (-(jnp.arange(half_rot, dtype=jnp.float32) * 2.0 / ROTARY))
    angle = direction * positions.astype(jnp.float32)[:, None] * freq[None, :]
    cosine = jnp.cos(angle)[:, None, :]
    sine = jnp.sin(angle)[:, None, :]
    first = tensor[..., :half_rot]
    second = tensor[..., half_rot:ROTARY]
    return jnp.concatenate(
        [first * cosine - second * sine, second * cosine + first * sine, tensor[..., ROTARY:]],
        axis=-1,
    )


def body(
    residual,
    norm_gain,
    norm_shift,
    qkv_weight,
    qkv_bias,
    dense_weight,
    dense_bias,
    inner_weight,
    inner_bias,
    outer_weight,
    outer_bias,
    cotangent,
    segment,
    ancestors,
    valid_slot,
):
    f32 = jnp.float32
    bf16 = jnp.bfloat16
    tp_size = lax.axis_size("tp")
    local_rows = residual.shape[0]
    group_rows = local_rows * tp_size
    head_cols = qkv_weight.shape[2]
    head_count = head_cols // HEAD_DIM
    reach_back = (TREE_LEN - 2) // group_rows + 1
    front_rows = reach_back * group_rows
    window = front_rows + group_rows
    block_rows = min(512, group_rows)
    block_count = group_rows // block_rows
    scaling = HEAD_DIM ** (-0.5)
    base_slot = lax.axis_index("fsdp") * group_rows
    vectors = (
        lax.all_gather(norm_gain, ("fsdp", "tp"), axis=0, tiled=True),
        lax.all_gather(norm_shift, ("fsdp", "tp"), axis=0, tiled=True),
        lax.all_gather(dense_bias, ("fsdp", "tp"), axis=0, tiled=True),
        lax.all_gather(outer_bias, ("fsdp", "tp"), axis=0, tiled=True),
    )
    gain_f = vectors[0].astype(f32)
    shift_f = vectors[1].astype(f32)
    bias_sum = vectors[2].astype(f32) + vectors[3].astype(f32)
    seg_front = jnp.concatenate([jnp.zeros((front_rows,), jnp.int32), segment])
    valid_front = jnp.concatenate([jnp.zeros((front_rows,), jnp.int32), valid_slot])
    query_slot = base_slot + jnp.arange(group_rows, dtype=jnp.int32)
    query_seg = lax.dynamic_slice_in_dim(segment, base_slot, group_rows)
    query_valid = lax.dynamic_slice_in_dim(valid_slot, base_slot, group_rows)
    key_slot = base_slot - front_rows + jnp.arange(window, dtype=jnp.int32)
    key_seg = lax.dynamic_slice_in_dim(seg_front, base_slot, window)
    key_valid = lax.dynamic_slice_in_dim(valid_front, base_slot, window)

    def allowed_for():
        return tree_allowed(
            query_seg, query_slot, query_valid, key_seg, key_slot, key_valid, ancestors
        )

    def count_keys(block_num):
        return jnp.sum(allowed_for().astype(jnp.int32), axis=1) - 1

    block_ids = jnp.arange(block_count, dtype=jnp.int32)
    positions = lax.map(count_keys, block_ids).reshape(group_rows)
    inputs_f = residual.astype(f32)
    normed_local = norm_rows(inputs_f, gain_f, shift_f).astype(bf16)

    def key_window(keys_own, values_own):
        key_parts = []
        value_parts = []
        for distance in range(reach_back, 0, -1):
            got_keys, got_values = passed_along((keys_own, values_own), "fsdp", distance)
            key_parts.append(got_keys)
            value_parts.append(got_values)
        return (
            jnp.concatenate(key_parts + [keys_own], axis=0),
            jnp.concatenate(value_parts + [values_own], axis=0),
        )

    def forward_pieces():
        gathered = (
            lax.all_gather(qkv_weight, "fsdp", axis=1, tiled=True),
            lax.all_gather(qkv_bias, "fsdp", axis=1, tiled=True),
            lax.all_gather(dense_weight, "fsdp", axis=1, tiled=True),
            lax.all_gather(inner_weight, "fsdp", axis=0, tiled=True),
            lax.all_gather(inner_bias, "fsdp", axis=0, tiled=True),
            lax.all_gather(outer_weight, "fsdp", axis=1, tiled=True),
        )
        normed = lax.all_gather(normed_local, "tp", axis=0, tiled=True)
        w_qkv = gathered[0]
        mixed = (
            jnp.einsum("td,sde->ste", normed, w_qkv, preferred_element_type=f32)
            + gathered[1].astype(f32)[:, None, :]
        )
        queries = rotate(mixed[0].reshape(group_rows, head_count, HEAD_DIM), positions, 1.0).astype(
            bf16
        )
        keys_own = (
            rotate(mixed[1].reshape(group_rows, head_count, HEAD_DIM), positions, 1.0)
            .astype(bf16)
            .reshape(group_rows, head_cols)
        )
        values_own = mixed[2].astype(bf16)
        keys_win, values_win = key_window(keys_own, values_own)
        keys_win = keys_win.reshape(window, head_count, HEAD_DIM)
        values_win = values_win.reshape(window, head_count, HEAD_DIM)

        def attend(block_num):
            scores = (
                jnp.einsum("qhe,khe->hqk", queries, keys_win, preferred_element_type=f32) * scaling
            )
            scores = jnp.where(allowed_for()[None], scores, -jnp.inf)
            top_score = jnp.max(scores, axis=-1, keepdims=True)
            expo = jnp.exp(scores - top_score)
            summed = jnp.sum(expo, axis=-1, keepdims=True)
            probs_low = (expo / summed).astype(bf16)
            attended = jnp.einsum("hqk,khe->qhe", probs_low, values_win, preferred_element_type=f32)
            return (attended, (top_score + jnp.log(summed))[..., 0])

        attended, log_sums = lax.map(attend, block_ids)
        attended = attended.reshape(group_rows, head_cols).astype(bf16)
        pre_act = jnp.dot(normed, gathered[3], preferred_element_type=f32) + gathered[4].astype(f32)
        activated = jax.nn.gelu(pre_act, approximate=True).astype(bf16)
        return (
            gathered,
            normed,
            queries,
            keys_win,
            values_win,
            attended,
            log_sums,
            pre_act,
            activated,
        )

    gathered, normed, queries, keys_win, values_win, attended, log_sums, pre_act, activated = (
        forward_pieces()
    )
    partial_rows = jnp.dot(attended, gathered[2], preferred_element_type=f32) + jnp.dot(
        activated, gathered[5], preferred_element_type=f32
    )
    summed_rows = lax.psum_scatter(partial_rows, "tp", scatter_dimension=0, tiled=True)
    output = (inputs_f + summed_rows + bias_sum).astype(bf16)
    out_bias_grad = jnp.sum(cotangent.astype(f32), axis=0)
    grad_rows = lax.all_gather(cotangent, "tp", axis=0, tiled=True)
    gathered, normed, queries, keys_win, values_win, attended, log_sums, pre_act, activated = (
        forward_pieces()
    )
    w_qkv = gathered[0]
    w_dense = gathered[2]
    w_inner = gathered[3]
    w_outer = gathered[5]
    outer_grad = jnp.einsum("tf,td->fd", activated, grad_rows, preferred_element_type=f32)
    act_grad = jnp.einsum("td,fd->tf", grad_rows, w_outer, preferred_element_type=f32)
    unused_value, gelu_pull = jax.vjp(
        lambda inputs_g: jax.nn.gelu(inputs_g, approximate=True), pre_act
    )
    pre_grad = gelu_pull(act_grad)[0].astype(bf16)
    inner_grad = jnp.einsum("td,tf->df", normed, pre_grad, preferred_element_type=f32)
    inner_bias_grad = jnp.sum(pre_grad.astype(f32), axis=0)
    normed_grad = jnp.einsum("tf,df->td", pre_grad, w_inner, preferred_element_type=f32)
    dense_grad = jnp.einsum("tc,td->cd", attended, grad_rows, preferred_element_type=f32)
    attn_grad = (
        jnp.einsum("td,cd->tc", grad_rows, w_dense, preferred_element_type=f32)
        .astype(bf16)
        .reshape(group_rows, head_count, HEAD_DIM)
    )

    def attend_back(carry, inputs_b):
        key_acc, value_acc = carry
        block_num, log_block = inputs_b
        scores = jnp.einsum("qhe,khe->hqk", queries, keys_win, preferred_element_type=f32) * scaling
        probs = jnp.where(allowed_for()[None], jnp.exp(scores - log_block[..., None]), 0.0)
        probs_low = probs.astype(bf16)
        prob_grad = jnp.einsum("qhe,khe->hqk", attn_grad, values_win, preferred_element_type=f32)
        row_dot = jnp.sum(probs * prob_grad, axis=-1, keepdims=True)
        score_grad = (probs * (prob_grad - row_dot)).astype(bf16)
        query_grad = (
            jnp.einsum("hqk,khe->qhe", score_grad, keys_win, preferred_element_type=f32) * scaling
        )
        key_part = (
            key_acc
            + jnp.einsum("hqk,qhe->khe", score_grad, queries, preferred_element_type=f32) * scaling
        )
        value_part = value_acc + jnp.einsum(
            "hqk,qhe->khe", probs_low, attn_grad, preferred_element_type=f32
        )
        key_acc = key_part
        value_acc = value_part
        return ((key_acc, value_acc), query_grad)

    zero_window = jnp.zeros((window, head_count, HEAD_DIM), f32)
    (key_acc, value_acc), query_grads = lax.scan(
        attend_back, (zero_window, zero_window), (block_ids, log_sums)
    )
    key_flat = key_acc.reshape(window, head_cols)
    value_flat = value_acc.reshape(window, head_cols)
    own_key = key_flat[front_rows:]
    own_value = value_flat[front_rows:]
    for distance in range(1, reach_back + 1):
        lower = front_rows - distance * group_rows
        got_key, got_value = passed_along(
            (key_flat[lower : lower + group_rows], value_flat[lower : lower + group_rows]),
            "fsdp",
            -distance,
        )
        own_key = own_key + got_key
        own_value = own_value + got_value
    query_pre = rotate(
        query_grads.reshape(group_rows, head_count, HEAD_DIM), positions, -1.0
    ).reshape(group_rows, head_cols)
    key_pre = rotate(own_key.reshape(group_rows, head_count, HEAD_DIM), positions, -1.0).reshape(
        group_rows, head_cols
    )
    qkv_grad = jnp.stack([query_pre, key_pre, own_value]).astype(bf16)
    qkv_weight_part = jnp.einsum("td,ste->sde", normed, qkv_grad, preferred_element_type=f32)
    qkv_bias_part = jnp.sum(qkv_grad.astype(f32), axis=1)
    normed_grad = normed_grad + jnp.einsum(
        "ste,sde->td", qkv_grad, w_qkv, preferred_element_type=f32
    )
    local_grad = lax.psum_scatter(normed_grad, "tp", scatter_dimension=0, tiled=True)
    unused_norm, norm_pull = jax.vjp(norm_rows, inputs_f, gain_f, shift_f)
    input_grad, gain_grad, shift_grad = norm_pull(local_grad)
    residual_grad = (cotangent.astype(f32) + input_grad).astype(bf16)
    weight_sums = (
        lax.psum_scatter(qkv_weight_part, "fsdp", scatter_dimension=1, tiled=True),
        lax.psum_scatter(qkv_bias_part, "fsdp", scatter_dimension=1, tiled=True),
        lax.psum_scatter(dense_grad, "fsdp", scatter_dimension=1, tiled=True),
        lax.psum_scatter(inner_grad, "fsdp", scatter_dimension=0, tiled=True),
        lax.psum_scatter(inner_bias_grad, "fsdp", scatter_dimension=0, tiled=True),
        lax.psum_scatter(outer_grad, "fsdp", scatter_dimension=1, tiled=True),
    )
    vector_sums = (
        lax.psum_scatter(gain_grad, ("fsdp", "tp"), scatter_dimension=0, tiled=True),
        lax.psum_scatter(shift_grad, ("fsdp", "tp"), scatter_dimension=0, tiled=True),
        lax.psum_scatter(out_bias_grad, ("fsdp", "tp"), scatter_dimension=0, tiled=True),
    )
    return (
        output,
        residual_grad,
        vector_sums[0],
        vector_sums[1],
        weight_sums[0],
        weight_sums[1],
        weight_sums[2],
        vector_sums[2],
        weight_sums[3],
        weight_sums[4],
        weight_sums[5],
        vector_sums[2],
    )


def solution(mesh):
    return jax.shard_map(
        body,
        mesh=mesh,
        in_specs=(
            P(("fsdp", "tp"), None),
            P(("fsdp", "tp")),
            P(("fsdp", "tp")),
            P(None, "fsdp", "tp"),
            P(None, ("tp", "fsdp")),
            P("tp", "fsdp"),
            P(("fsdp", "tp")),
            P("fsdp", "tp"),
            P(("tp", "fsdp")),
            P("tp", "fsdp"),
            P(("fsdp", "tp")),
            P(("fsdp", "tp"), None),
            P(),
            P(),
            P(),
        ),
        out_specs=(
            P(("fsdp", "tp"), None),
            P(("fsdp", "tp"), None),
            P(("fsdp", "tp")),
            P(("fsdp", "tp")),
            P(None, "fsdp", "tp"),
            P(None, ("tp", "fsdp")),
            P("tp", "fsdp"),
            P(("fsdp", "tp")),
            P("fsdp", "tp"),
            P(("tp", "fsdp")),
            P("tp", "fsdp"),
            P(("fsdp", "tp")),
        ),
        check_vma=False,
    )
```

profile of v0, /device:TPU:0, one launch (start us, length us, event | category | flops | bytes accessed | tf_op | source)
XLA Modules:
  0.0 1016.9 jit_solution(10757736382496534110)
XLA Ops:
  10.7 42.2 %all-reduce.11 = (bf16[2048]{0:T(1024)(128)(2,1)S(1)}, bf16[2048]{0:T(1024)(128)(2,1)S(1)}, bf16[2048]{0:T(1024)(128)(2,1)}, bf16[2048]{0:T(1024)(128)(2,1)}) all-reduce(bf16[2048]{0:T(1024)(128)(2,1)S(1)} %dynamic-update-slice.1, bf16[2048]{0:T(1024)(128)(2,1)S(1)} %dynamic-update-slice, ...), channel_id=1, replica_groups=mesh['fsdp'=8,'tp'=4] {'fsdp','tp'}, use_global_device_ids=true, to_apply=%add.3 | all-reduce | flops 8192 | bytes 32768
  65.6 10.2 %all-gather = bf16[8,64,3]{1,2,0:T(4,128)(2,1)S(1)} all-gather(bf16[1,64,3]{1,2,0:T(4,128)(2,1)S(1)} %bitcast.110), channel_id=1, replica_groups=mesh['fsdp'=8,'tp'=4] {'fsdp'}, dimensions={0}, use_global_device_ids=true | all-gather | bytes 3456 | tf_op jit(solution)/shard_map/all_gather | solution.py:132
  75.9 7.9 all-gather.1
  85.4 19.4 %all-gather.9.cloned.1.call-done = bf16[512,2048]{1,0:T(8,128)(2,1)} async-done(((bf16[128,2048]{1,0:T(8,128)(2,1)}), bf16[512,2048]{1,0:T(8,128)(2,1)}) %all-gather.9.cloned.1.call-update) | async-done | bytes 2097168 | tf_op jit(solution)/shard_map/all_gather | solution.py:138
  104.8 47.9 %all-gather.11.cloned.1.call-done = bf16[3,2048,512]{1,2,0:T(8,128)(2,1)} async-done(((bf16[3,256,512]{1,2,0:T(8,128)(2,1)}), bf16[3,2048,512]{1,2,0:T(8,128)(2,1)}) %all-gather.11.cloned.1.call-update) | async-done | bytes 6291472 | tf_op jit(solution)/shard_map/all_gather | solution.py:131
  167.4 32.8 %all-gather.19.cloned.1.call-done = bf16[512,2048]{1,0:T(8,128)(2,1)} async-done(((bf16[128,2048]{1,0:T(8,128)(2,1)}), bf16[512,2048]{1,0:T(8,128)(2,1)}) %all-gather.19.cloned.1.call-update) | async-done | bytes 2097168 | tf_op jit(solution)/shard_map/all_gather | solution.py:194
  200.2 28.7 %all-gather.13.cloned.1.call-done = bf16[512,2048]{1,0:T(8,128)(2,1)} async-done(((bf16[512,256]{1,0:T(8,128)(2,1)}), bf16[512,2048]{1,0:T(8,128)(2,1)}) %all-gather.13.cloned.1.call-update) | async-done | bytes 2097168 | tf_op jit(solution)/shard_map/all_gather | solution.py:133
  239.4 11.9 %select_reduce_fusion = (f32[8,512]{1,0:T(8,128)S(1)}, f32[8,512,1536]{2,1,0:T(8,128)}) fusion(pred[512,1536]{1,0:T(8,128)(4,1)S(1)} %get-tuple-element.236, bf16[512,8,64]{0,2,1:T(8,128)(2,1)S(1)} %maximum_convert_fusion, bf16[512,8,64]{0,2,1:T(8,128)(2,1)} %bitcast.14, bf16[512,8,64]{0,2,1:T(8,128)(2,1)} %bitcast.13, bf16[512,8,32]{0,2,1:T(8,128)(2,1)S(1)} %slice.202, ...), kind=kOutput, calls=%fused_computation.5 | convolution fusion | flops 830468096 | bytes 28065792 | tf_op jit(solution)/shard_map/while/body/eval_jaxpr/qhe,khe->hqk/dot_general | solution.py:159
  251.3 11.6 %fusion = f32[8,512]{1,0:T(8,128)S(1)} fusion(f32[8,512,1536]{2,1,0:T(8,128)} %get-tuple-element.268, f32[8,512]{1,0:T(8,128)S(1)} %get-tuple-element.267, pred[512,1536]{1,0:T(8,128)(4,1)S(1)} %get-tuple-element.236), kind=kLoop, calls=%fused_computation.6 | loop fusion | flops 25161728 | bytes 25985024 | tf_op jit(solution)/shard_map/while/body/eval_jaxpr/reduce_sum | solution.py:164
  263.5 19.6 %multiply_reduce_fusion = (f32[8,512]{1,0:T(8,128)S(1)}, f32[8,512,1536]{2,1,0:T(8,128)}) fusion(f32[8,512,1536]{2,1,0:T(8,128)} %get-tuple-element.268, f32[8,512]{1,0:T(8,128)S(1)} %log_add_fusion, pred[512,1536]{1,0:T(8,128)(4,1)S(1)} %get-tuple-element.236, bf16[512,8,64]{0,2,1:T(8,128)(2,1)S(1)} %bitcast.100, bf16[1536,8,64]{0,2,1:T(8,128)(2,1)S(1)} %bitcast.82), kind=kOutput, calls=%fused_computation.1 | convolution fusion | flops 836759552 | bytes 53248000 | tf_op jit(solution)/shard_map/while/body/eval_jaxpr/qhe,khe->hqk/dot_general | solution.py:224
  283.1 17.4 %multiply_convert_fusion = bf16[8,512,1536]{2,1,0:T(8,128)(2,1)S(1)} fusion(f32[8,512,1536]{2,1,0:T(8,128)} %get-tuple-element.270, f32[8,512,1536]{2,1,0:T(8,128)} %get-tuple-element.268, f32[8,512]{1,0:T(8,128)S(1)} %get-tuple-element.269, f32[8,512]{1,0:T(8,128)S(1)} %log_add_fusion, pred[512,1536]{1,0:T(8,128)(4,1)S(1)} %get-tuple-element.236), kind=kLoop, calls=%fused_computation | loop fusion | flops 37748736 | bytes 63733760 | tf_op jit(solution)/shard_map/while/body/eval_jaxpr/convert_element_type | solution.py:226
  309.8 10.9 %fusion.14 = f32[1536,8,64]{0,2,1:T(8,128)S(1)} fusion(bf16[512,8,64]{0,2,1:T(8,128)(2,1)S(1)} %bitcast.101, f32[8,512,1536]{2,1,0:T(8,128)} %get-tuple-element.268, f32[8,512]{1,0:T(8,128)S(1)} %log_add_fusion, pred[512,1536]{1,0:T(8,128)(4,1)S(1)} %get-tuple-element.236), kind=kOutput, calls=%fused_computation.26 | convolution fusion | flops 830472192 | bytes 29638656 | tf_op jit(solution)/shard_map/while/body/eval_jaxpr/hqk,qhe->khe/dot_general | solution.py:234
  328.8 9.0 fusion.26
  340.4 22.6 %collective-permute-done.5 = f32[512,512]{0,1:T(8,128)} collective-permute-done((f32[512,512]{0,1:T(8,128)}, f32[512,512]{0,1:T(8,128)}, u32[]{:S(2)}, u32[]{:S(2)}) %collective-permute-start.5) | collective-permute-done | bytes 1048608 | tf_op jit(solution)/shard_map/ppermute | solution.py:17
  374.3 11.8 %collective-permute-done.7 = f32[512,512]{1,0:T(8,128)} collective-permute-done((f32[512,512]{1,0:T(8,128)}, f32[512,512]{1,0:T(8,128)}, u32[]{:S(2)}, u32[]{:S(2)}) %collective-permute-start.7) | collective-permute-done | bytes 1048608 | tf_op jit(solution)/shard_map/ppermute | solution.py:17
  391.0 8.8 reduce-scatter.12.cloned.1.call-start
  399.8 10.5 %fusion.61 = f32[512,2048]{1,0:T(8,128)} fusion(bf16[512,2048]{1,0:T(8,128)(2,1)} %all-gather.9.cloned.1.call-done, bf16[2048,2048]{1,0:T(8,128)(2,1)} %all-gather.15.cloned.1.call-done), kind=kOutput, calls=%fused_computation.123 | convolution fusion | flops 4294967296 | bytes 14680064 | tf_op jit(solution)/shard_map/dot_general | solution.py:171
  410.4 9.8 all-gather.17.cloned.1.call-done
  420.2 12.2 %convert_reduce_fusion = (f32[2048]{0:T(1024)S(1)}, bf16[512,2048]{1,0:T(8,128)(2,1)S(1)}) fusion(f32[512,2048]{1,0:T(8,128)} %fusion.61, f32[2048]{0:T(1024)S(1)} %bitcast.106, bf16[512,2048]{1,0:T(8,128)(2,1)} %all-gather.19.cloned.1.call-done, bf16[2048,2048]{1,0:T(8,128)(2,1)} %all-gather.17.cloned.1.call-done), kind=kOutput, calls=%fused_computation.22 | convolution fusion | flops 4319082496 | bytes 16793600 | tf_op jit(solution)/shard_map/td,fd->tf/dot_general | solution.py:203
  446.0 11.6 %fusion.27 = bf16[8,64,512]{2,1,0:T(8,128)(2,1)S(1)} fusion(bf16[1536,8,64]{0,2,1:T(8,128)(2,1)S(1)} %bitcast.83, f32[8,512,1536]{2,1,0:T(8,128)} %get-tuple-element.268, f32[8,512]{1,0:T(8,128)S(1)} %copy-done.19, f32[8,512]{1,0:T(8,128)S(1)} %get-tuple-element.267, pred[512,1536]{1,0:T(8,128)(4,1)S(1)} %get-tuple-element.236), kind=kOutput, calls=%fused_computation.51 | convolution fusion | flops 837025792 | bytes 28082176 | tf_op jit(solution)/shard_map/while/body/eval_jaxpr/hqk,khe->qhe/dot_general | solution.py:166
  457.6 8.1 fusion.54
  470.3 8.0 convolution_bitcast_fusion
  483.5 12.6 %fusion.64 = f32[2048,2048]{1,0:T(8,128)} fusion(bf16[512,2048]{1,0:T(8,128)(2,1)} %all-gather.9.cloned.1.call-done, bf16[512,2048]{1,0:T(8,128)(2,1)} %copy-done.37), kind=kOutput, calls=%fused_computation.126 | convolution fusion | flops 4294967296 | bytes 20971520 | tf_op jit(solution)/shard_map/td,tf->df/dot_general | solution.py:208
  496.1 11.9 %fusion.53 = f32[2048,2048]{1,0:T(8,128)} fusion(bf16[512,2048]{1,0:T(8,128)(2,1)S(1)} %copy-done.11, f32[512,2048]{1,0:T(8,128)} %fusion.61, f32[2048]{0:T(1024)S(1)} %bitcast.108), kind=kOutput, calls=%fused_computation.116 | convolution fusion | flops 4305453056 | bytes 23076864 | tf_op jit(solution)/shard_map/tf,td->fd/dot_general | solution.py:202
  511.4 14.1 %all-reduce.9 = f32[2048]{0:T(1024)S(1)} all-reduce(f32[2048]{0:T(1024)S(1)} %get-tuple-element.233), channel_id=11, replica_groups=mesh['fsdp'=8,'tp'=4] {'fsdp'}, use_global_device_ids=true, to_apply=%region_23.24.clone | all-reduce | flops 2048 | bytes 16384
  526.1 10.6 %reduce-scatter.12.cloned.1.call-done = f32[128,2048]{1,0:T(8,128)} async-done(((f32[512,2048]{1,0:T(8,128)}), f32[128,2048]{1,0:T(8,128)}) %reduce-scatter.12.cloned.1.call-update) | async-done | bytes 1048592 | tf_op jit(solution)/shard_map/reduce_scatter | solution.py:270
  540.0 76.3 %reduce-scatter.10.cloned.1.call-done = f32[128,2048]{1,0:T(8,128)} async-done(((f32[512,2048]{1,0:T(8,128)}), f32[128,2048]{1,0:T(8,128)}) %reduce-scatter.10.cloned.1.call-update) | async-done | bytes 1048592 | tf_op jit(solution)/shard_map/reduce_scatter | solution.py:191
  619.5 41.2 %all-reduce.10 = (f32[2048]{0:T(1024)S(1)}, f32[2048]{0:T(1024)S(1)}, f32[2048]{0:T(1024)S(1)}) all-reduce(f32[2048]{0:T(1024)S(1)} %get-tuple-element.222, f32[2048]{0:T(1024)S(1)} %get-tuple-element.224, f32[2048]{0:T(1024)S(1)} %get-tuple-element.253), channel_id=4, replica_groups=mesh['fsdp'=8,'tp'=4] {'fsdp','tp'}, use_global_device_ids=true, to_apply=%region_12.13.clone | all-reduce | flops 6144 | bytes 49152
  661.9 51.6 %reduce-scatter.14.cloned.1.call-done = f32[3,256,512]{1,2,0:T(8,128)} async-done(((f32[3,2048,512]{1,2,0:T(8,128)}), f32[3,256,512]{1,2,0:T(8,128)}) %reduce-scatter.14.cloned.1.call-update) | async-done | bytes 1572880 | tf_op jit(solution)/shard_map/reduce_scatter | solution.py:275
  716.6 52.6 %reduce-scatter.16.cloned.1.call-done = f32[512,256]{1,0:T(8,128)} async-done(((f32[512,2048]{1,0:T(8,128)}), f32[512,256]{1,0:T(8,128)}) %reduce-scatter.16.cloned.1.call-update) | async-done | bytes 524304 | tf_op jit(solution)/shard_map/reduce_scatter | solution.py:277
  769.2 120.0 %reduce-scatter.18.cloned.1.call-done = f32[256,2048]{1,0:T(8,128)} async-done(((f32[2048,2048]{1,0:T(8,128)}), f32[256,2048]{1,0:T(8,128)}) %reduce-scatter.18.cloned.1.call-update) | async-done | bytes 2097168 | tf_op jit(solution)/shard_map/reduce_scatter | solution.py:278
  889.2 120.2 %reduce-scatter.20.cloned.1.call-done = f32[2048,256]{1,0:T(8,128)} async-done(((f32[2048,2048]{1,0:T(8,128)}), f32[2048,256]{1,0:T(8,128)}) %reduce-scatter.20.cloned.1.call-update) | async-done | bytes 2097168 | tf_op jit(solution)/shard_map/reduce_scatter | solution.py:280
  (198 shorter events, 117.2 us)
Async XLA Ops:
  7.2 56.0 %copy-start.21 = (s32[4096]{0:T(1024)S(1)}, s32[4096]{0:T(1024)}, u32[]{:S(2)}) copy-start(s32[4096]{0:T(1024)} %param.27) | copy-start | bytes 49156
  7.2 56.1 %copy-start.20 = (s32[4096]{0:T(1024)S(1)}, s32[4096]{0:T(1024)}, u32[]{:S(2)}) copy-start(s32[4096]{0:T(1024)} %param.29) | copy-start | bytes 49156
  7.2 56.3 %copy-start.29 = (s32[39,3]{0,1:T(4,128)S(1)}, s32[39,3]{0,1:T(4,128)}, u32[]{:S(2)}) copy-start(s32[39,3]{0,1:T(4,128)} %param.28) | copy-start | bytes 1408
  7.2 97.6 %all-gather.9.cloned.1.call-start = ((), (), s32[]{:S(2)}) async-start(), calls=%async_computation.7 | async-start | bytes 2621440 | tf_op jit(solution)/shard_map/all_gather | solution.py:138
  58.3 94.3 %all-gather.11.cloned.1.call-start = ((), (), s32[]{:S(2)}) async-start(), calls=%async_computation.8 | async-start | bytes 7077888 | tf_op jit(solution)/shard_map/all_gather | solution.py:131
  60.7 139.5 %all-gather.19.cloned.1.call-start = ((), (), s32[]{:S(2)}) async-start(), calls=%async_computation.13 | async-start | bytes 2621440 | tf_op jit(solution)/shard_map/all_gather | solution.py:194
  61.4 167.5 %all-gather.13.cloned.1.call-start = ((), (), s32[]{:S(2)}) async-start(), calls=%async_computation.9 | async-start | bytes 2359296 | tf_op jit(solution)/shard_map/all_gather | solution.py:133
  62.0 337.9 %all-gather.15.cloned.1.call-start = ((), (), s32[]{:S(2)}) async-start(), calls=%async_computation.10 | async-start | bytes 9437184 | tf_op jit(solution)/shard_map/all_gather | solution.py:134
  62.6 357.7 %all-gather.17.cloned.1.call-start = ((), (), s32[]{:S(2)}) async-start(), calls=%async_computation.11 | async-start | bytes 9437184 | tf_op jit(solution)/shard_map/all_gather | solution.py:136
  63.1 446.8 %reduce-scatter.22.cloned.1.call-start = ((), (), s32[]{:S(2)}) async-start(), calls=%async_computation.19 | async-start | bytes 294912
  160.5 78.9 %copy-start.14 = (bf16[512,8,64]{0,2,1:T(8,128)(2,1)}, bf16[512,8,64]{0,2,1:T(8,128)(2,1)S(1)}, u32[]{:S(2)}) copy-start(bf16[512,8,64]{0,2,1:T(8,128)(2,1)S(1)} %maximum_convert_fusion) | copy-start | bytes 1572868
  160.6 78.8 %collective-permute-start.2 = (bf16[512,512]{0,1:T(8,128)(2,1)S(1)}, bf16[512,512]{0,1:T(8,128)(2,1)}, u32[]{:S(2)}, u32[]{:S(2)}) collective-permute-start(bf16[512,512]{0,1:T(8,128)(2,1)S(1)} %bitcast.97), channel_id=1, source_target_pairs={{0,8},{4,12},{8,16},{12,20},{16,24},{20,28},{1,9},{5,13},{9,17},{1... | collective-permute-start | bytes 1572872 | tf_op jit(solution)/shard_map/ppermute | solution.py:17
  164.7 74.7 %collective-permute-start.3 = (bf16[512,512]{0,1:T(8,128)(2,1)S(1)}, bf16[512,512]{0,1:T(8,128)(2,1)}, u32[]{:S(2)}, u32[]{:S(2)}) collective-permute-start(bf16[512,512]{0,1:T(8,128)(2,1)S(1)} %bitcast.98), channel_id=1, source_target_pairs={{0,4},{4,8},{8,12},{12,16},{16,20},{20,24},{24,28},{1,5},{5,9},{9,... | collective-permute-start | bytes 1572872 | tf_op jit(solution)/shard_map/ppermute | solution.py:17
  233.8 29.2 %collective-permute-start = (bf16[512,512]{0,1:T(8,128)(2,1)S(1)}, bf16[512,512]{0,1:T(8,128)(2,1)S(1)}, u32[]{:S(2)}, u32[]{:S(2)}) collective-permute-start(bf16[512,512]{0,1:T(8,128)(2,1)S(1)} %fusion.41), channel_id=1, source_target_pairs={{0,8},{4,12},{8,16},{12,20},{16,24},{20,28},{1,9},{5,13},{9,17},{1... | collective-permute-start | bytes 1572872 | tf_op jit(solution)/shard_map/ppermute | solution.py:17
  237.2 25.8 %collective-permute-start.1 = (bf16[512,512]{0,1:T(8,128)(2,1)S(1)}, bf16[512,512]{0,1:T(8,128)(2,1)S(1)}, u32[]{:S(2)}, u32[]{:S(2)}) collective-permute-start(bf16[512,512]{0,1:T(8,128)(2,1)S(1)} %fusion.41), channel_id=1, source_target_pairs={{0,4},{4,8},{8,12},{12,16},{16,20},{20,24},{24,28},{1,5},{5,9},{9,... | collective-permute-start | bytes 1572872 | tf_op jit(solution)/shard_map/ppermute | solution.py:17
  307.2 33.2 %collective-permute-start.4 = (f32[512,512]{0,1:T(8,128)}, f32[512,512]{0,1:T(8,128)}, u32[]{:S(2)}, u32[]{:S(2)}) collective-permute-start(f32[512,512]{0,1:T(8,128)} %bitcast.23), channel_id=1, source_target_pairs={{4,0},{8,4},{12,8},{16,12},{20,16},{24,20},{28,24},{5,1},{9,5},{13... | collective-permute-start | bytes 3145736 | tf_op jit(solution)/shard_map/ppermute | solution.py:17
  308.5 54.5 %collective-permute-start.5 = (f32[512,512]{0,1:T(8,128)}, f32[512,512]{0,1:T(8,128)}, u32[]{:S(2)}, u32[]{:S(2)}) collective-permute-start(f32[512,512]{0,1:T(8,128)} %bitcast.24), channel_id=1, source_target_pairs={{8,0},{12,4},{16,8},{20,12},{24,16},{28,20},{9,1},{13,5},{17,9},{2... | collective-permute-start | bytes 3145736 | tf_op jit(solution)/shard_map/ppermute | solution.py:17
  324.9 49.4 %collective-permute-start.6 = (f32[512,512]{1,0:T(8,128)}, f32[512,512]{1,0:T(8,128)}, u32[]{:S(2)}, u32[]{:S(2)}) collective-permute-start(f32[512,512]{1,0:T(8,128)} %copy.71), channel_id=1, source_target_pairs={{4,0},{8,4},{12,8},{16,12},{20,16},{24,20},{28,24},{5,1},{9,5},{13... | collective-permute-start | bytes 3145736 | tf_op jit(solution)/shard_map/ppermute | solution.py:17
  327.5 58.6 %collective-permute-start.7 = (f32[512,512]{1,0:T(8,128)}, f32[512,512]{1,0:T(8,128)}, u32[]{:S(2)}, u32[]{:S(2)}) collective-permute-start(f32[512,512]{1,0:T(8,128)} %copy.73), channel_id=1, source_target_pairs={{8,0},{12,4},{16,8},{20,12},{24,16},{28,20},{9,1},{13,5},{17,9},{2... | collective-permute-start | bytes 3145736 | tf_op jit(solution)/shard_map/ppermute | solution.py:17
  391.0 29.2 %copy-start.24 = (f32[8,1,256]{2,1,0:T(1,128)S(1)}, f32[8,1,256]{2,1,0:T(1,128)}, u32[]{:S(2)}) copy-start(f32[8,1,256]{2,1,0:T(1,128)} %convert_element_type.155) | copy-start | bytes 24580
  391.0 145.7 %reduce-scatter.12.cloned.1.call-start = ((), (), s32[]{:S(2)}) async-start(), calls=%async_computation.14 | async-start | bytes 5242880 | tf_op jit(solution)/shard_map/reduce_scatter | solution.py:270
  445.3 171.0 %reduce-scatter.10.cloned.1.call-start = ((), (), s32[]{:S(2)}) async-start(), calls=%async_computation.12 | async-start | bytes 5242880 | tf_op jit(solution)/shard_map/reduce_scatter | solution.py:191
  469.1 244.5 %reduce-scatter.14.cloned.1.call-start = ((), (), s32[]{:S(2)}) async-start(), calls=%async_computation.15 | async-start | bytes 14155776 | tf_op jit(solution)/shard_map/reduce_scatter | solution.py:275
  478.3 290.9 %reduce-scatter.16.cloned.1.call-start = ((), (), s32[]{:S(2)}) async-start(), calls=%async_computation.16 | async-start | bytes 4718592 | tf_op jit(solution)/shard_map/reduce_scatter | solution.py:277
  483.2 406.1 %reduce-scatter.18.cloned.1.call-start = ((), (), s32[]{:S(2)}) async-start(), calls=%async_computation.17 | async-start | bytes 18874368 | tf_op jit(solution)/shard_map/reduce_scatter | solution.py:278
  496.1 513.3 %reduce-scatter.20.cloned.1.call-start = ((), (), s32[]{:S(2)}) async-start(), calls=%async_computation.18 | async-start | bytes 18874368 | tf_op jit(solution)/shard_map/reduce_scatter | solution.py:280
  508.0 28.7 %copy-start.1 = (bf16[128,2048]{1,0:T(8,128)(2,1)S(1)}, bf16[128,2048]{1,0:T(8,128)(2,1)}, u32[]{:S(2)}) copy-start(bf16[128,2048]{1,0:T(8,128)(2,1)} %param.15) | copy-start | bytes 1572868
  508.0 28.7 %copy-start.17 = (f32[2048]{0:T(1024)S(1)}, f32[2048]{0:T(1024)}, u32[]{:S(2)}) copy-start(f32[2048]{0:T(1024)} %copy-done.16) | copy-start | bytes 24580
  508.0 30.2 %copy-start.32 = (f32[128]{0:T(128)S(1)}, f32[128]{0:T(128)}, u32[]{:S(2)}) copy-start(f32[128]{0:T(128)} %copy-done.31) | copy-start | bytes 1540
  508.0 30.2 %copy-start.26 = (f32[128]{0:T(128)S(1)}, f32[128]{0:T(128)}, u32[]{:S(2)}) copy-start(f32[128]{0:T(128)} %copy-done.25) | copy-start | bytes 1540
  508.1 108.2 %copy-start.12 = (bf16[128,2048]{1,0:T(8,128)(2,1)S(1)}, bf16[128,2048]{1,0:T(8,128)(2,1)}, u32[]{:S(2)}) copy-start(bf16[128,2048]{1,0:T(8,128)(2,1)} %param.26) | copy-start | bytes 1572868
  660.7 349.2 %copy-start.36 = (f32[64]{0:T(128)}, f32[64]{0:T(128)S(1)}, u32[]{:S(2)}) copy-start(f32[64]{0:T(128)S(1)} %dynamic-slice.2) | copy-start | bytes 772
  (28 other events, 196.8 us)
Sparse Core Ops, SparseCore 0:
  58.4 46.3 all-gather.8
  107.2 45.3 all-gather.10
  154.2 45.9 all-gather.18
  201.9 26.8 all-gather.12
  230.6 64.4 all-gather.14
  296.8 123.3 all-gather.16
  423.8 33.6 reduce-scatter.21
  459.9 76.7 reduce-scatter.11
  539.0 77.2 reduce-scatter.9
  620.0 93.4 reduce-scatter.13
  717.9 51.3 reduce-scatter.15
  773.2 115.9 reduce-scatter.17
  893.4 115.9 reduce-scatter.19
where the time goes:
time: 1020 us
  waiting for transfers between devices  607 us (60%)
  matrix products  158 us (15%)
  blocking collectives  116 us (11%)
  other arithmetic  54 us (5%)
  local copies, waits for them, and re-layouts  40 us (4%)
  starting transfers between devices  27.1 us (3%)
  between operations  15.8 us (2%)
    reduce_scatter x1, waiting for transfers between devices, body(): lax.psum_scatter(outer_grad, 'fsdp', scatter_dimension=1, tiled=True)  120 us
    reduce_scatter x1, waiting for transfers between devices, body(): lax.psum_scatter(inner_grad, 'fsdp', scatter_dimension=0, tiled=True)  120 us
    unnamed x3, blocking collectives  97.5 us
    reduce_scatter x1, waiting for transfers between devices, body(): lax.psum_scatter(partial_rows, 'tp', scatter_dimension=0, tiled=True)  76.3 us
    reduce_scatter x1, waiting for transfers between devices, body(): lax.psum_scatter(dense_grad, 'fsdp', scatter_dimension=1, tiled=True)  52.6 us
    reduce_scatter x1, waiting for transfers between devices, body(): lax.psum_scatter(qkv_weight_part, 'fsdp', scatter_dimension=1, tiled=True)  51.6 us
    all_gather x1, waiting for transfers between devices, forward_pieces(): lax.all_gather(qkv_weight, 'fsdp', axis=1, tiled=True)  47.9 us
    ppermute x8, waiting for transfers between devices, passed_along(): lax.ppermute(value, axis, [(source, source + steps) for source in range(i...  34.4 us
  transfers between devices with their start and end apart: 21, of which 13 were waited for; matrix products, arithmetic and copies ran while one was open for 23% of the time, Pallas kernels for 0%

commit v1 on v0

v1 whole, which is shorter than its diff:
```python
import jax
import jax.numpy as jnp
from jax import lax
from jax.experimental import pallas as pl
from jax.experimental.pallas import tpu as pltpu
from jax.sharding import PartitionSpec as P

HEAD_DIM = 64
ROTARY = 32
TREE_LEN = 1024
EPSILON = 1e-05
LANES = 128
QROWS = 256
KROWS = 256
MASKED = -1e30

f32 = jnp.float32
bf16 = jnp.bfloat16

NN = (((1,), (0,)), ((), ()))
NT = (((1,), (1,)), ((), ()))
TN = (((0,), (0,)), ((), ()))


def dot(left, right, dims=NN):
    return lax.dot_general(left, right, dims, preferred_element_type=f32)


class Layout:
    def __init__(self):
        self.fs = lax.axis_size("fsdp")
        self.tp = lax.axis_size("tp")
        chips = self.fs // 2
        self.A = 2
        self.B = chips // 2
        index = lax.axis_index("fsdp")
        self.index = index
        self.core = index % 2
        self.chip = index // 2
        self.a = self.chip // self.B
        self.b = self.chip % self.B
        self.z = lax.axis_index("tp")
        self.is0 = self.core == 0

    def blocks(self):
        A, B = self.A, self.B
        first = [(0, i, j) for i in range(A) for j in range(B)]
        second = [(1, i, j) for j in range(B) for i in range(A)]
        return first + second

    def offsets(self):
        out = []
        for core, i, j in self.blocks():
            chip = ((self.a + i) % self.A) * self.B + (self.b + j) % self.B
            out.append(chip * 2 + core)
        return jnp.stack(out).astype(jnp.int32)

    def pair_of(self, fn):
        A, B = self.A, self.B
        pairs = []
        for a in range(A):
            for b in range(B):
                for c in range(2):
                    pairs.append(((a * B + b) * 2 + c, fn(a, b, c)))
        return pairs

    def over_core(self, value):
        B = self.B
        return lax.ppermute(value, "fsdp", self.pair_of(lambda a, b, c: (a * B + b) * 2 + 1 - c))

    def along_a(self, value, steps):
        A, B = self.A, self.B
        return lax.ppermute(
            value, "fsdp", self.pair_of(lambda a, b, c: (((a + steps) % A) * B + b) * 2 + c)
        )

    def along_b(self, value, steps):
        B = self.B
        return lax.ppermute(
            value, "fsdp", self.pair_of(lambda a, b, c: (a * B + (b + steps) % B) * 2 + c)
        )

    def along_z(self, value, steps):
        n = self.tp
        return lax.ppermute(value, "tp", [(s, (s + steps) % n) for s in range(n)])

    def with_partner(self, value, axis, bit):
        size = self.fs if axis == "fsdp" else self.tp
        return lax.ppermute(value, axis, [(s, s ^ bit) for s in range(size)])

    def bits(self):
        out = []
        for axis, size, index in (("tp", self.tp, self.z), ("fsdp", self.fs, self.index)):
            bit = 1
            while bit < size:
                out.append((axis, bit, (index // bit) % 2 == 1))
                bit *= 2
        return out

    def by_core(self, own, other):
        return jnp.where(self.is0, own, other), jnp.where(self.is0, other, own)


def gather_pieces(lay, first, second):
    A, B = lay.A, lay.B
    p_row = jnp.stack([first] + [lay.along_b(first, -j) for j in range(1, B)])
    q_row = jnp.stack([second] + [lay.along_a(second, -i) for i in range(1, A)])
    p_far = [lay.along_a(p_row, -i) for i in range(1, A)]
    q_far = [lay.along_b(q_row, -j) for j in range(1, B)]
    p_far = p_far[0] if A == 2 else jnp.concatenate(p_far)
    q_far = q_far[0] if B == 2 else jnp.concatenate(q_far)
    return (p_row, p_far, q_row, q_far)


def scatter_pieces(lay, near, far):
    A, B = lay.A, lay.B
    p_row, q_row = near
    p_far, q_far = far
    p_sum = p_row.astype(f32)
    for i in range(1, A):
        p_sum = p_sum + lay.along_a(p_far[(i - 1) * B : i * B], i).astype(f32)
    q_sum = q_row.astype(f32)
    for j in range(1, B):
        q_sum = q_sum + lay.along_b(q_far[(j - 1) * A : j * A], j).astype(f32)
    p_out = p_sum[0]
    for j in range(1, B):
        p_out = p_out + lay.along_b(p_sum[j].astype(bf16), j).astype(f32)
    q_out = q_sum[0]
    for i in range(1, A):
        q_out = q_out + lay.along_a(q_sum[i].astype(bf16), i).astype(f32)
    return p_out, q_out


def small_gather(lay, row):
    held = row
    for axis, bit, upper in lay.bits():
        got = lay.with_partner(held, axis, bit)
        held = jnp.concatenate([jnp.where(upper, got, held), jnp.where(upper, held, got)])
    return held


def small_scatter(lay, rows):
    held = rows
    for axis, bit, upper in reversed(lay.bits()):
        size = held.shape[0] // 2
        low, high = held[:size], held[size:]
        got = lay.with_partner(jnp.where(upper, low, high), axis, bit)
        held = jnp.where(upper, high, low) + got
    return held


def ring_gather(lay, own):
    n = lay.tp
    half = own.shape[0] // 2
    held = {0: own}
    up, down = own, own
    for step in range(1, n // 2):
        up = lay.along_z(up, 1)
        down = lay.along_z(down, -1)
        held[n - step] = up
        held[step] = down
    low = lay.along_z(up[:half], 1)
    high = lay.along_z(down[half:], -1)
    held[n // 2] = jnp.concatenate([low, high])
    ordered = jnp.concatenate([held[m % n] for m in range(2 * n - 1)])
    start = ((n - lay.z) % n) * own.shape[0]
    return lax.dynamic_slice_in_dim(ordered, start, n * own.shape[0])


def ring_scatter(lay, rows):
    n = lay.tp
    size = rows.shape[0] // n
    half = size // 2
    twice = jnp.concatenate([rows, rows])
    turned = lax.dynamic_slice_in_dim(twice, lay.z * size, n * size)

    def block(m):
        return turned[(m % n) * size : (m % n) * size + size]

    far = block(n // 2)
    up_low = lay.along_z(far[:half], 1)
    down_high = lay.along_z(far[half:], -1)
    up = jnp.concatenate(
        [block(n // 2 - 1)[:half].astype(f32) + up_low.astype(f32), block(n // 2 - 1)[half:].astype(f32)]
    )
    low = n // 2 + 1
    down = jnp.concatenate(
        [block(low)[:half].astype(f32), block(low)[half:].astype(f32) + down_high.astype(f32)]
    )
    for step in range(1, n // 2):
        up_got = lay.along_z(up.astype(bf16), 1)
        down_got = lay.along_z(down.astype(bf16), -1)
        up = block(n // 2 - 1 - step).astype(f32) + up_got.astype(f32)
        down = block(low + step).astype(f32) + down_got.astype(f32)
    return up + down - block(0).astype(f32)


def params(**kw):
    return pltpu.CompilerParams(vmem_limit_bytes=56 * 1024 * 1024, **kw)


def cost(flops, bytes_accessed, transcendentals=0):
    return pl.CostEstimate(
        flops=int(flops), bytes_accessed=int(bytes_accessed), transcendentals=int(transcendentals)
    )


def whole(array):
    rank = len(array.shape)
    return pl.BlockSpec(array.shape, lambda *_: (0,) * rank)


def listed(refs):
    return [(ref, k) for ref in refs for k in range(ref.shape[0])]


def column(offs, n, width):
    return pl.ds(pl.multiple_of(offs[n] * width, width), width)


def turn(value, keep, ahead, behind):
    half = ROTARY // 2
    parts = []
    for chunk in range(value.shape[1] // LANES):
        v = value[:, chunk * LANES : (chunk + 1) * LANES]
        parts.append(
            v * keep
            + pltpu.roll(v, LANES - half, 1) * ahead
            + pltpu.roll(v, half, 1) * behind
        )
    return parts[0] if len(parts) == 1 else jnp.concatenate(parts, axis=1)


def project(lay, offs, rows, gain, shift, bias, tables, pieces):
    T, D = rows.shape
    H = bias.shape[1] // 3
    BD = D // lay.fs
    blocks = 2 * lay.A * lay.B

    def kernel(offs, rows_ref, gain_ref, shift_ref, bias_ref, tab_ref, p0, p1, q0, q1, normed_ref, q_ref, kv_ref):
        x = rows_ref[...].astype(f32)
        mean = jnp.sum(x, axis=1, keepdims=True) * (1.0 / D)
        x = x - mean
        var = jnp.sum(x * x, axis=1, keepdims=True) * (1.0 / D)
        normed = x * lax.rsqrt(var + EPSILON) * gain_ref[...] + shift_ref[...]
        normed_ref[...] = normed.astype(bf16)
        weights = listed((p0, p1, q0, q1))
        keep, ahead, behind = tab_ref[0], tab_ref[1], tab_ref[2]
        for s in range(3):
            total = bias_ref[:, s * H : (s + 1) * H]
            for n, (ref, k) in enumerate(weights):
                total = total + dot(normed_ref[:, column(offs, n, BD)], ref[k, s * BD : (s + 1) * BD, :])
            if s == 0:
                q_ref[...] = (turn(total, keep, ahead, behind).astype(bf16) * (HEAD_DIM**-0.5)).astype(bf16)
            elif s == 1:
                kv_ref[0] = turn(total, keep, ahead, behind).astype(bf16)
            else:
                kv_ref[1] = total.astype(bf16)

    R = QROWS
    return pl.pallas_call(
        kernel,
        out_shape=(
            jax.ShapeDtypeStruct((T, D), bf16),
            jax.ShapeDtypeStruct((T, H), bf16),
            jax.ShapeDtypeStruct((2, T, H), bf16),
        ),
        grid_spec=pltpu.PrefetchScalarGridSpec(
            num_scalar_prefetch=1,
            grid=(T // R,),
            in_specs=[
                pl.BlockSpec((R, D), lambda t, o: (t, 0)),
                whole(gain),
                whole(shift),
                whole(bias),
                pl.BlockSpec((3, R, LANES), lambda t, o: (0, t, 0)),
            ]
            + [whole(p) for p in pieces],
            out_specs=[
                pl.BlockSpec((R, D), lambda t, o: (t, 0)),
                pl.BlockSpec((R, H), lambda t, o: (t, 0)),
                pl.BlockSpec((2, R, H), lambda t, o: (0, t, 0)),
            ],
        ),
        compiler_params=params(),
        cost_estimate=cost(2 * T * D * 3 * H, 2 * T * D * 2 + 8 * T * H + 2 * D * 4 * H),
        name="project",
    )(offs, rows, gain, shift, bias, tables, *pieces)


def attention(lay, offs, queries, kv_own, kv_prev, cot, pieces, paths, codes, tables):
    T, H = queries.shape
    D = cot.shape[1]
    BD = D // lay.fs
    QB = T // QROWS
    SPAN = T + QROWS
    KB = SPAN // KROWS
    pairs = H // LANES
    scaling = HEAD_DIM**-0.5

    def kernel(
        offs, q_ref, own_ref, prev_ref, cot_ref, path_ref, code_ref, tab_ref, p0, p1, q0, q1,
        att_ref, dq_ref, dprev_ref, down_ref,
        k_sc, v_sc, kt_sc, vt_sc, dk_sc, dv_sc, bias_sc, e_sc, g_sc, p_sc, d_sc,
    ):
        pair = pl.program_id(0)
        i = pl.program_id(1)

        @pl.when(i == 0)
        def _():
            k_sc[:T] = prev_ref[0]
            k_sc[T:] = own_ref[0]
            v_sc[:T] = prev_ref[1]
            v_sc[T:] = own_ref[1]
            for c in range(2 * T // KROWS):
                rows = slice(c * KROWS, (c + 1) * KROWS)
                kt_sc[:, rows] = k_sc[rows].astype(f32).T.astype(bf16)
                vt_sc[:, rows] = v_sc[rows].astype(f32).T.astype(bf16)
            dk_sc[...] = jnp.zeros_like(dk_sc)
            dv_sc[...] = jnp.zeros_like(dv_sc)

        base = pl.multiple_of(i * QROWS, QROWS)
        head_rows = pl.ds(pl.multiple_of(pair * LANES, LANES), LANES)
        grad = jnp.zeros((QROWS, LANES), f32)
        for n, (ref, k) in enumerate(listed((p0, p1, q0, q1))):
            rows = pl.ds(pl.multiple_of(3 * BD + pair * LANES, LANES), LANES)
            grad = grad + dot(cot_ref[:, column(offs, n, BD)], ref[k, rows, :], NT)
        grad = grad.astype(bf16)
        queries_pair = q_ref[...]

        key_at = lax.broadcasted_iota(jnp.int32, (KROWS, QROWS), 0)
        query_at = lax.broadcasted_iota(jnp.int32, (KROWS, QROWS), 1) + T
        path0, path1, path2 = path_ref[0:1, :], path_ref[1:2, :], path_ref[2:3, :]
        for c in range(KB):
            start = pl.multiple_of(base + c * KROWS, KROWS)
            code = code_ref[pl.ds(start, KROWS), :]
            code = jnp.concatenate([code, code], axis=1)
            at = key_at + c * KROWS
            linked = (code == path0) | (code == path1) | (code == path2)
            seen = (linked & (at <= query_at)) | (at == query_at)
            bias_sc[c] = jnp.where(seen, 0.0, MASKED)

        lane = lax.broadcasted_iota(jnp.int32, (QROWS, LANES), 1)
        att_t, dq_t = [], []
        for head in range(2):
            mine = (lane >= head * HEAD_DIM) & (lane < (head + 1) * HEAD_DIM)
            qh = jnp.where(mine, queries_pair, jnp.zeros_like(queries_pair))
            gh = jnp.where(mine, grad, jnp.zeros_like(grad))
            top = jnp.full((1, QROWS), MASKED, f32)
            for c in range(KB):
                start = pl.multiple_of(base + c * KROWS, KROWS)
                s = dot(k_sc[pl.ds(start, KROWS), :], qh, NT) + bias_sc[c]
                e_sc[c] = s
                top = jnp.maximum(top, jnp.max(s, axis=0, keepdims=True))
            summed = jnp.zeros((1, QROWS), f32)
            mixed = jnp.zeros((1, QROWS), f32)
            for c in range(KB):
                start = pl.multiple_of(base + c * KROWS, KROWS)
                e = jnp.exp(e_sc[c] - top)
                g = dot(v_sc[pl.ds(start, KROWS), :], gh, NT)
                e_sc[c] = e
                g_sc[c] = g
                summed = summed + jnp.sum(e, axis=0, keepdims=True)
                mixed = mixed + jnp.sum(e * g, axis=0, keepdims=True)
            inverse = 1.0 / summed
            mixed = mixed * inverse
            for c in range(KB):
                probs = e_sc[c] * inverse
                p_sc[c * KROWS : (c + 1) * KROWS] = probs.astype(bf16)
                d_sc[c * KROWS : (c + 1) * KROWS] = (probs * (g_sc[c] - mixed)).astype(bf16)
            span = pl.ds(base, SPAN)
            hrow = slice(head * HEAD_DIM, (head + 1) * HEAD_DIM)
            att_t.append(dot(vt_sc[hrow, span], p_sc[...]))
            dq_t.append(dot(kt_sc[hrow, span], d_sc[...]))
            dv_sc[span, :] += dot(p_sc[...], gh)
            dk_sc[span, :] += dot(d_sc[...], qh)
        att_ref[...] = jnp.concatenate(att_t, axis=0).T.astype(bf16)
        dq = jnp.concatenate(dq_t, axis=0).T * scaling
        dq_ref[...] = turn(dq, tab_ref[0], -tab_ref[1], -tab_ref[2]).astype(bf16)

        @pl.when(i == QB - 1)
        def _():
            dprev_ref[0] = dk_sc[:T].astype(bf16)
            dprev_ref[1] = dv_sc[:T].astype(bf16)
            down_ref[0] = dk_sc[T:]
            down_ref[1] = dv_sc[T:]

    elements = (H // HEAD_DIM) * T * SPAN
    return pl.pallas_call(
        kernel,
        out_shape=(
            jax.ShapeDtypeStruct((T, H), bf16),
            jax.ShapeDtypeStruct((T, H), bf16),
            jax.ShapeDtypeStruct((2, T, H), bf16),
            jax.ShapeDtypeStruct((2, T, H), f32),
        ),
        grid_spec=pltpu.PrefetchScalarGridSpec(
            num_scalar_prefetch=1,
            grid=(pairs, QB),
            in_specs=[
                pl.BlockSpec((QROWS, LANES), lambda p, i, o: (i, p)),
                pl.BlockSpec((2, T, LANES), lambda p, i, o: (0, 0, p)),
                pl.BlockSpec((2, T, LANES), lambda p, i, o: (0, 0, p)),
                pl.BlockSpec((QROWS, D), lambda p, i, o: (i, 0)),
                pl.BlockSpec((8, QROWS), lambda p, i, o: (0, i)),
                whole(codes),
                pl.BlockSpec((3, QROWS, LANES), lambda p, i, o: (0, i, 0)),
            ]
            + [whole(p) for p in pieces],
            out_specs=[
                pl.BlockSpec((QROWS, LANES), lambda p, i, o: (i, p)),
                pl.BlockSpec((QROWS, LANES), lambda p, i, o: (i, p)),
                pl.BlockSpec((2, T, LANES), lambda p, i, o: (0, 0, p)),
                pl.BlockSpec((2, T, LANES), lambda p, i, o: (0, 0, p)),
            ],
            scratch_shapes=[
                pltpu.VMEM((2 * T, LANES), bf16),
                pltpu.VMEM((2 * T, LANES), bf16),
                pltpu.VMEM((LANES, 2 * T), bf16),
                pltpu.VMEM((LANES, 2 * T), bf16),
                pltpu.VMEM((2 * T, LANES), f32),
                pltpu.VMEM((2 * T, LANES), f32),
                pltpu.VMEM((KB, KROWS, QROWS), f32),
                pltpu.VMEM((KB, KROWS, QROWS), f32),
                pltpu.VMEM((KB, KROWS, QROWS), f32),
                pltpu.VMEM((SPAN, QROWS), bf16),
                pltpu.VMEM((SPAN, QROWS), bf16),
            ],
        ),
        compiler_params=params(),
        cost_estimate=cost(elements * 64 * 12 * 4, 2 * T * D + 20 * T * H, elements),
        name="attention",
    )(offs, queries, kv_own, kv_prev, cot, paths, codes, tables, *pieces)


def inner_forward(lay, offs, normed, bias, pieces):
    T, D = normed.shape
    F = bias.shape[1]
    BD = D // lay.fs
    R = QROWS

    def kernel(offs, x_ref, bias_ref, p0, p1, q0, q1, act_ref, slope_ref):
        u = bias_ref[...]
        for n, (ref, k) in enumerate(listed((p0, p1, q0, q1))):
            u = u + dot(x_ref[:, column(offs, n, BD)], ref[k])
        scale = (2.0 / jnp.pi) ** 0.5
        square = u * u
        t = jnp.tanh(scale * (u + 0.044715 * (square * u)))
        act_ref[...] = (0.5 * u * (1.0 + t)).astype(bf16)
        slope = 0.5 * (1.0 + t) + 0.5 * u * (1.0 - t * t) * (scale * (1.0 + (3 * 0.044715) * square))
        slope_ref[...] = slope

    return pl.pallas_call(
        kernel,
        out_shape=(jax.ShapeDtypeStruct((T, F), bf16), jax.ShapeDtypeStruct((T, F), f32)),
        grid_spec=pltpu.PrefetchScalarGridSpec(
            num_scalar_prefetch=1,
            grid=(T // R,),
            in_specs=[pl.BlockSpec((R, D), lambda t, o: (t, 0)), whole(bias)] + [whole(p) for p in pieces],
            out_specs=[
                pl.BlockSpec((R, F), lambda t, o: (t, 0)),
                pl.BlockSpec((R, F), lambda t, o: (t, 0)),
            ],
        ),
        compiler_params=params(),
        cost_estimate=cost(2 * T * D * F, 2 * T * D + 2 * D * F + 6 * T * F, T * F),
        name="inner_forward",
    )(offs, normed, bias, *pieces)


def inner_backward(lay, offs, cot, slope, pieces):
    T, D = cot.shape
    F = slope.shape[1]
    BD = D // lay.fs
    R = QROWS

    def kernel(offs, c_ref, slope_ref, p0, p1, q0, q1, grad_ref, bias_ref):
        total = jnp.zeros((R, F), f32)
        for n, (ref, k) in enumerate(listed((p0, p1, q0, q1))):
            total = total + dot(c_ref[:, column(offs, n, BD)], ref[k], NT)
        grad = (total * slope_ref[...]).astype(bf16)
        grad_ref[...] = grad

        @pl.when(pl.program_id(0) == 0)
        def _():
            bias_ref[...] = jnp.zeros_like(bias_ref)

        bias_ref[...] += jnp.sum(grad.astype(f32), axis=0, keepdims=True)

    return pl.pallas_call(
        kernel,
        out_shape=(jax.ShapeDtypeStruct((T, F), bf16), jax.ShapeDtypeStruct((1, F), f32)),
        grid_spec=pltpu.PrefetchScalarGridSpec(
            num_scalar_prefetch=1,
            grid=(T // R,),
            in_specs=[
                pl.BlockSpec((R, D), lambda t, o: (t, 0)),
                pl.BlockSpec((R, F), lambda t, o: (t, 0)),
            ]
            + [whole(p) for p in pieces],
            out_specs=[
                pl.BlockSpec((R, F), lambda t, o: (t, 0)),
                pl.BlockSpec((1, F), lambda t, o: (0, 0)),
            ],
        ),
        compiler_params=params(),
        cost_estimate=cost(2 * T * D * F, 2 * T * D + 2 * D * F + 6 * T * F),
        name="inner_backward",
    )(offs, cot, slope, *pieces)


def block_grads(lay, offs, wide, narrow, picks, wide_first, name):
    T, D = wide.shape
    F = narrow.shape[1]
    BD = D // lay.fs
    shape = (BD, F) if wide_first else (F, BD)

    def kernel(offs, wide_ref, narrow_ref, *rest):
        outs = rest[: len(picks)]
        held = rest[len(picks)] if len(rest) > len(picks) else None
        if held is not None:
            held[...] = narrow_ref[...].T
        for ref, chosen in zip(outs, picks):
            for k, n in enumerate(chosen):
                block = wide_ref[:, column(offs, n, BD)]
                if wide_first:
                    ref[k] = dot(block.T, narrow_ref[...]).astype(bf16)
                else:
                    ref[k] = dot(held[...], block).astype(bf16)

    count = sum(len(chosen) for chosen in picks)
    return pl.pallas_call(
        kernel,
        out_shape=tuple(jax.ShapeDtypeStruct((len(chosen),) + shape, bf16) for chosen in picks),
        grid_spec=pltpu.PrefetchScalarGridSpec(
            num_scalar_prefetch=1,
            grid=(1,),
            in_specs=[whole(wide), whole(narrow)],
            out_specs=[
                pl.BlockSpec((len(chosen),) + shape, lambda t, o: (0, 0, 0)) for chosen in picks
            ],
            scratch_shapes=[] if wide_first else [pltpu.VMEM((F, T), bf16)],
        ),
        compiler_params=params(),
        cost_estimate=cost(2 * T * BD * F * count, 2 * T * D + 2 * T * F + 2 * BD * F * count),
        name=name,
    )(offs, wide, narrow)


def attn_weight_grads(lay, offs, normed, cot, dq, dkv, attended, picks, name):
    T, D = normed.shape
    H = dq.shape[1]
    BD = D // lay.fs

    def kernel(offs, x_ref, c_ref, dq_ref, dkv_ref, att_ref, *outs):
        att = att_ref[...].T
        for ref, chosen in zip(outs, picks):
            for k, n in enumerate(chosen):
                block = x_ref[:, column(offs, n, BD)].T
                ref[k, :BD] = dot(block, dq_ref[...]).astype(bf16)
                ref[k, BD : 2 * BD] = dot(block, dkv_ref[0]).astype(bf16)
                ref[k, 2 * BD : 3 * BD] = dot(block, dkv_ref[1]).astype(bf16)
                ref[k, 3 * BD :] = dot(att, c_ref[:, column(offs, n, BD)]).astype(bf16)

    count = sum(len(chosen) for chosen in picks)
    shape = (3 * BD + H, H)
    return pl.pallas_call(
        kernel,
        out_shape=tuple(jax.ShapeDtypeStruct((len(chosen),) + shape, bf16) for chosen in picks),
        grid_spec=pltpu.PrefetchScalarGridSpec(
            num_scalar_prefetch=1,
            grid=(1,),
            in_specs=[whole(v) for v in (normed, cot, dq, dkv, attended)],
            out_specs=[
                pl.BlockSpec((len(chosen),) + shape, lambda t, o: (0, 0, 0)) for chosen in picks
            ],
        ),
        compiler_params=params(),
        cost_estimate=cost(8 * T * BD * H * count, 4 * T * D + 8 * T * H + 8 * BD * H * count),
        name=name,
    )(offs, normed, cot, dq, dkv, attended)


def output_rows(lay, offs, attended, activated, attn_pieces, outer_pieces, D):
    T, F = activated.shape
    H = attended.shape[1]
    BD = D // lay.fs
    R = QROWS

    def kernel(offs, att_ref, act_ref, a0, a1, b0, b1, p0, p1, q0, q1, out_ref):
        small = listed((a0, a1, b0, b1))
        large = listed((p0, p1, q0, q1))
        for n in range(len(small)):
            (sref, sk), (lref, lk) = small[n], large[n]
            total = dot(act_ref[...], lref[lk]) + dot(att_ref[...], sref[sk, 3 * BD : 3 * BD + H, :])
            out_ref[:, column(offs, n, BD)] = total.astype(bf16)

    return pl.pallas_call(
        kernel,
        out_shape=jax.ShapeDtypeStruct((T, D), bf16),
        grid_spec=pltpu.PrefetchScalarGridSpec(
            num_scalar_prefetch=1,
            grid=(T // R,),
            in_specs=[
                pl.BlockSpec((R, H), lambda t, o: (t, 0)),
                pl.BlockSpec((R, F), lambda t, o: (t, 0)),
            ]
            + [whole(p) for p in attn_pieces]
            + [whole(p) for p in outer_pieces],
            out_specs=pl.BlockSpec((R, D), lambda t, o: (t, 0)),
        ),
        compiler_params=params(),
        cost_estimate=cost(2 * T * D * (F + H), 2 * T * (D + F + H) + 2 * D * (F + H)),
        name="output_rows",
    )(offs, attended, activated, *attn_pieces, *outer_pieces)


def normed_grads(lay, offs, pre_grad, dq, dkv, rows, attn_pieces, inner_pieces):
    T, D = rows.shape
    F = pre_grad.shape[1]
    H = dq.shape[1]
    BD = D // lay.fs
    R = QROWS

    def kernel(offs, pre_ref, dq_ref, dkv_ref, rows_ref, a0, a1, b0, b1, p0, p1, q0, q1, out_ref, sums_ref, stand_sc):
        @pl.when(pl.program_id(0) == 0)
        def _():
            sums_ref[...] = jnp.zeros_like(sums_ref)

        x = rows_ref[...].astype(f32)
        mean = jnp.sum(x, axis=1, keepdims=True) * (1.0 / D)
        x = x - mean
        var = jnp.sum(x * x, axis=1, keepdims=True) * (1.0 / D)
        stand_sc[...] = x * lax.rsqrt(var + EPSILON)
        small = listed((a0, a1, b0, b1))
        large = listed((p0, p1, q0, q1))
        for n in range(len(small)):
            (sref, sk), (lref, lk) = small[n], large[n]
            at = column(offs, n, BD)
            total = (
                dot(pre_ref[...], lref[lk], NT)
                + dot(dq_ref[...], sref[sk, :BD, :], NT)
                + dot(dkv_ref[0], sref[sk, BD : 2 * BD, :], NT)
                + dot(dkv_ref[1], sref[sk, 2 * BD : 3 * BD, :], NT)
            )
            out_ref[:, at] = total.astype(bf16)
            sums_ref[0:1, at] += jnp.sum(total * stand_sc[:, at], axis=0, keepdims=True)
            sums_ref[1:2, at] += jnp.sum(total, axis=0, keepdims=True)

    return pl.pallas_call(
        kernel,
        out_shape=(jax.ShapeDtypeStruct((T, D), bf16), jax.ShapeDtypeStruct((8, D), f32)),
        grid_spec=pltpu.PrefetchScalarGridSpec(
            num_scalar_prefetch=1,
            grid=(T // R,),
            in_specs=[
                pl.BlockSpec((R, F), lambda t, o: (t, 0)),
                pl.BlockSpec((R, H), lambda t, o: (t, 0)),
                pl.BlockSpec((2, R, H), lambda t, o: (0, t, 0)),
                pl.BlockSpec((R, D), lambda t, o: (t, 0)),
            ]
            + [whole(p) for p in attn_pieces]
            + [whole(p) for p in inner_pieces],
            out_specs=[
                pl.BlockSpec((R, D), lambda t, o: (t, 0)),
                pl.BlockSpec((8, D), lambda t, o: (0, 0)),
            ],
            scratch_shapes=[pltpu.VMEM((R, D), f32)],
        ),
        compiler_params=params(),
        cost_estimate=cost(2 * T * D * (F + 3 * H), 2 * T * (2 * D + F + 3 * H) + 2 * D * (F + 3 * H)),
        name="normed_grads",
    )(offs, pre_grad, dq, dkv, rows, *attn_pieces, *inner_pieces)


def key_value_grads(dkv_own, dkv_got, dq, tables):
    _, T, H = dkv_own.shape

    def kernel(own_ref, got_ref, dq_ref, tab_ref, out_ref, bias_ref):
        dk = own_ref[0] + got_ref[0].astype(f32)
        dv = own_ref[1] + got_ref[1].astype(f32)
        dk = turn(dk, tab_ref[0], -tab_ref[1], -tab_ref[2]).astype(bf16)
        dv = dv.astype(bf16)
        out_ref[0] = dk
        out_ref[1] = dv
        bias_ref[...] = jnp.zeros_like(bias_ref)
        bias_ref[0:1] = jnp.sum(dq_ref[...].astype(f32), axis=0, keepdims=True)
        bias_ref[1:2] = jnp.sum(dk.astype(f32), axis=0, keepdims=True)
        bias_ref[2:3] = jnp.sum(dv.astype(f32), axis=0, keepdims=True)

    return pl.pallas_call(
        kernel,
        out_shape=(jax.ShapeDtypeStruct((2, T, H), bf16), jax.ShapeDtypeStruct((8, H), f32)),
        compiler_params=params(),
        cost_estimate=cost(10 * T * H, 20 * T * H),
        name="key_value_grads",
    )(dkv_own, dkv_got, dq, tables)


def body(
    residual,
    norm_gain,
    norm_shift,
    qkv_weight,
    qkv_bias,
    dense_weight,
    dense_bias,
    inner_weight,
    inner_bias,
    outer_weight,
    outer_bias,
    cotangent,
    segment,
    ancestors,
    valid_slot,
):
    lay = Layout()
    fs, tp = lay.fs, lay.tp
    D = residual.shape[1]
    T = residual.shape[0] * tp * 2
    HC = qkv_weight.shape[2] // 2
    FC = inner_weight.shape[1] // 2
    BD = qkv_weight.shape[1]
    assert T >= TREE_LEN - 1 and BD == HC
    offs = lay.offsets()
    is0 = lay.is0

    half = (qkv_weight[:, :, :HC].reshape(3 * BD, HC), qkv_weight[:, :, HC:].reshape(3 * BD, HC))
    attn_half = (
        jnp.concatenate([half[0], dense_weight[:HC]]),
        jnp.concatenate([half[1], dense_weight[HC:]]),
    )
    inner_half = (inner_weight[:, :FC], inner_weight[:, FC:])
    outer_half = (outer_weight[:FC], outer_weight[FC:])

    def gathered(pair):
        keep, send = lay.by_core(*pair)
        first, second = lay.by_core(keep, lay.over_core(send))
        return gather_pieces(lay, first, second)

    attn_pieces = gathered(attn_half)
    inner_pieces = gathered(inner_half)
    outer_pieces = gathered(outer_half)

    def chip_rows(block):
        own = ring_gather(lay, block)
        first, second = lay.by_core(own, lay.over_core(own))
        return jnp.concatenate([first, second])

    rows = chip_rows(residual)
    cot = chip_rows(cotangent)

    flat = jnp.concatenate(
        [norm_gain, norm_shift, dense_bias, outer_bias, qkv_bias.reshape(-1), inner_bias]
    )
    vectors = small_gather(lay, flat.reshape(1, -1)).astype(f32)
    n_small = norm_gain.shape[0]
    gain = vectors[:, :n_small].reshape(1, D)
    shift = vectors[:, n_small : 2 * n_small].reshape(1, D)
    bias_sum = (vectors[:, 2 * n_small : 3 * n_small] + vectors[:, 3 * n_small : 4 * n_small]).reshape(1, D)
    mine = lax.dynamic_index_in_dim(vectors.reshape(fs, tp, -1), lay.z, axis=1, keepdims=False)
    n_qkv = qkv_bias.shape[1]
    mine = lax.dynamic_slice_in_dim(mine, lay.core * (fs // 2), fs // 2, axis=0)
    my_qkv_bias = (
        mine[:, 4 * n_small : 4 * n_small + 3 * n_qkv]
        .reshape(fs // 2, 3, n_qkv)
        .transpose(1, 0, 2)
        .reshape(1, 3 * HC)
    )
    my_inner_bias = mine[:, 4 * n_small + 3 * n_qkv :].reshape(1, FC)

    base_slot = lay.chip * T
    seg_front = jnp.concatenate([jnp.zeros((T,), jnp.int32), segment])
    valid_front = jnp.concatenate([jnp.zeros((T,), jnp.int32), valid_slot])
    window_seg = lax.dynamic_slice_in_dim(seg_front, base_slot, 2 * T)
    window_valid = lax.dynamic_slice_in_dim(valid_front, base_slot, 2 * T)
    codes = jnp.where(window_valid == 1, window_seg, -1)
    own_seg, own_valid = window_seg[T:], window_valid[T:]
    seg_ids = jnp.arange(ancestors.shape[0], dtype=jnp.int32)
    onehot = (own_seg[None, :] == seg_ids[:, None]).astype(jnp.int32)
    paths = jnp.sum(onehot[None, :, :] * ancestors.T[:, :, None], axis=1)
    paths = jnp.where(own_valid[None, :] == 1, paths, -2)
    key_at = jnp.arange(2 * T, dtype=jnp.int32)[:, None]
    query_at = T + jnp.arange(T, dtype=jnp.int32)[None, :]
    code_col = codes[:, None]
    linked = (code_col == paths[0:1]) | (code_col == paths[1:2]) | (code_col == paths[2:3])
    allowed = (linked & (key_at <= query_at)) | (key_at == query_at)
    positions = jnp.sum(allowed.astype(jnp.int32), axis=0) - 1
    paths8 = jnp.concatenate([paths, jnp.zeros((5, T), jnp.int32)])
    codes_wide = jnp.broadcast_to(code_col, (2 * T, LANES))

    half_rot = ROTARY // 2
    freq = 10000.0 ** (-(jnp.arange(half_rot, dtype=f32) * 2.0 / ROTARY))
    angle = positions.astype(f32)[:, None] * freq[None, :]
    cosine, sine = jnp.cos(angle), jnp.sin(angle)
    still = jnp.ones((T, HEAD_DIM - ROTARY), f32)
    none16 = jnp.zeros((T, half_rot), f32)
    none32 = jnp.zeros((T, HEAD_DIM - ROTARY), f32)
    twice = LANES // HEAD_DIM
    tables = jnp.stack(
        [
            jnp.concatenate([cosine, cosine, still] * twice, axis=1),
            jnp.concatenate([-sine, none16, none32] * twice, axis=1),
            jnp.concatenate([none16, sine, none32] * twice, axis=1),
        ]
    )

    normed, queries, kv_own = project(lay, offs, rows, gain, shift, my_qkv_bias, tables, attn_pieces)
    forward_pairs = [(s, s + 2) for s in range(fs - 2)]
    backward_pairs = [(s + 2, s) for s in range(fs - 2)]
    kv_prev = lax.ppermute(kv_own, "fsdp", forward_pairs)
    attended, dq, dkv_prev, dkv_own = attention(
        lay, offs, queries, kv_own, kv_prev, cot, attn_pieces, paths8, codes_wide, tables
    )
    dkv_got = lax.ppermute(dkv_prev, "fsdp", backward_pairs)

    A, B = lay.A, lay.B
    near = (tuple(range(B)), tuple(A * B + m for m in range(A)))
    far = (tuple(range(B, A * B)), tuple(A * B + m for m in range(A, A * B)))

    activated, slope = inner_forward(lay, offs, normed, my_inner_bias, inner_pieces)
    outer_far = block_grads(lay, offs, cot, activated, far, False, "outer_grads_far")
    outer_near = block_grads(lay, offs, cot, activated, near, False, "outer_grads_near")
    outer_sums = scatter_pieces(lay, outer_near, outer_far)

    pre_grad, inner_bias_part = inner_backward(lay, offs, cot, slope, outer_pieces)
    inner_far = block_grads(lay, offs, normed, pre_grad, far, True, "inner_grads_far")
    inner_near = block_grads(lay, offs, normed, pre_grad, near, True, "inner_grads_near")
    inner_sums = scatter_pieces(lay, inner_near, inner_far)

    dkv, qkv_bias_part = key_value_grads(dkv_own, dkv_got, dq, tables)
    attn_far = attn_weight_grads(lay, offs, normed, cot, dq, dkv, attended, far, "attn_grads_far")
    attn_near = attn_weight_grads(lay, offs, normed, cot, dq, dkv, attended, near, "attn_grads_near")
    attn_sums = scatter_pieces(lay, attn_near, attn_far)

    def swapped(sums):
        first, second = sums
        keep = jnp.where(is0, first, second)
        send = jnp.where(is0, second, first)
        return lay.by_core(keep, lay.over_core(send))

    low, high = swapped(outer_sums)
    outer_weight_grad = jnp.concatenate([low, high], axis=0)
    low, high = swapped(inner_sums)
    inner_weight_grad = jnp.concatenate([low, high], axis=1)
    low, high = swapped(attn_sums)
    qkv_weight_grad = jnp.concatenate(
        [low[: 3 * BD].reshape(3, BD, HC), high[: 3 * BD].reshape(3, BD, HC)], axis=2
    )
    dense_weight_grad = jnp.concatenate([low[3 * BD :], high[3 * BD :]], axis=0)

    def to_rows(partial):
        group = T // 2
        keep = jnp.where(is0, partial[:group], partial[group:])
        send = jnp.where(is0, partial[group:], partial[:group])
        summed = keep.astype(f32) + lay.over_core(send).astype(f32)
        return ring_scatter(lay, summed.astype(bf16))

    partial_out = output_rows(lay, offs, attended, activated, attn_pieces, outer_pieces, D)
    inputs_f = residual.astype(f32)
    output = (inputs_f + to_rows(partial_out) + bias_sum).astype(bf16)

    partial_grad, norm_sums = normed_grads(
        lay, offs, pre_grad, dq, dkv, rows, attn_pieces, inner_pieces
    )
    row_mean = jnp.mean(inputs_f, axis=-1, keepdims=True)
    centered = inputs_f - row_mean
    scale = lax.rsqrt(jnp.mean(centered * centered, axis=-1, keepdims=True) + EPSILON)
    stand = centered * scale
    cot_f = cotangent.astype(f32)
    e = to_rows(partial_grad) * gain
    e_mean = jnp.mean(e, axis=-1, keepdims=True)
    es_mean = jnp.mean(e * stand, axis=-1, keepdims=True)
    residual_grad = (cot_f + (e - e_mean - stand * es_mean) * scale).astype(bf16)

    out_bias_part = jnp.sum(cot_f, axis=0)
    wide = [v.reshape(fs, tp, n_small) for v in (norm_sums[0], norm_sums[1], out_bias_part)]
    heads = qkv_bias_part[:3].reshape(3, fs // 2, n_qkv).transpose(1, 0, 2).reshape(fs // 2, 3 * n_qkv)
    narrow = jnp.concatenate([heads, inner_bias_part.reshape(fs // 2, -1)], axis=1)
    blank = jnp.zeros_like(narrow)
    placed = jnp.concatenate([jnp.where(is0, narrow, blank), jnp.where(is0, blank, narrow)])
    mine_z = (jnp.arange(tp) == lay.z)[None, :, None]
    placed = jnp.where(mine_z, placed[:, None, :], 0.0)
    buffer = jnp.concatenate(wide + [placed], axis=2).reshape(fs * tp, -1)
    summed = small_scatter(lay, buffer)[0]
    gain_grad = summed[:n_small]
    shift_grad = summed[n_small : 2 * n_small]
    out_bias_grad = summed[2 * n_small : 3 * n_small]
    qkv_bias_grad = summed[3 * n_small : 3 * n_small + 3 * n_qkv].reshape(3, n_qkv)
    inner_bias_grad = summed[3 * n_small + 3 * n_qkv :]

    return (
        output,
        residual_grad,
        gain_grad,
        shift_grad,
        qkv_weight_grad,
        qkv_bias_grad,
        dense_weight_grad,
        out_bias_grad,
        inner_weight_grad,
        inner_bias_grad,
        outer_weight_grad,
        out_bias_grad,
    )


def solution(mesh):
    return jax.shard_map(
        body,
        mesh=mesh,
        in_specs=(
            P(("fsdp", "tp"), None),
            P(("fsdp", "tp")),
            P(("fsdp", "tp")),
            P(None, "fsdp", "tp"),
            P(None, ("tp", "fsdp")),
            P("tp", "fsdp"),
            P(("fsdp", "tp")),
            P("fsdp", "tp"),
            P(("tp", "fsdp")),
            P("tp", "fsdp"),
            P(("fsdp", "tp")),
            P(("fsdp", "tp"), None),
            P(),
            P(),
            P(),
        ),
        out_specs=(
            P(("fsdp", "tp"), None),
            P(("fsdp", "tp"), None),
            P(("fsdp", "tp")),
            P(("fsdp", "tp")),
            P(None, "fsdp", "tp"),
            P(None, ("tp", "fsdp")),
            P("tp", "fsdp"),
            P(("fsdp", "tp")),
            P("fsdp", "tp"),
            P(("tp", "fsdp")),
            P("tp", "fsdp"),
            P(("fsdp", "tp")),
        ),
        check_vma=False,
    )
```

time: 1020 us -> 520 us (0.51)
  waiting for transfers between devices: 607 us -> 154 us
  matrix products: 158 us -> 0 us
  Pallas kernels: 0 us -> 149 us
  blocking collectives: 116 us -> 0 us
  starting transfers between devices: 27.1 us -> 77 us
  other arithmetic: 54 us -> 82.6 us
  between operations: 15.8 us -> 2.27 us
    reduce_scatter x6 -> x0, waiting for transfers between devices: 431 us -> none  [the longest x1 120 us: body(): lax.psum_scatter(outer_grad, 'fsdp', scatter_dimension=1, tiled=True)]
    dot_general x18 -> x0, matrix products: 158 us -> none  [the longest x1 19.6 us: attend_back(): jnp.einsum('qhe,khe->hqk', attn_grad, values_win, preferred_element_type=...]
    pallas_call x0 -> x13, Pallas kernels: none -> 149 us  [the longest x1 37.4 us: attention(): pl.pallas_call(kernel, out_shape=(jax.ShapeDtypeStruct((T, H), bf16), jax...]
    all_gather x6 -> x0, waiting for transfers between devices: 139 us -> none  [the longest x1 47.9 us: forward_pieces(): lax.all_gather(qkv_weight, 'fsdp', axis=1, tiled=True)]
    ppermute x8 -> x62, waiting for transfers between devices: 34.4 us -> 154 us  [the longest x16 68.7 us: along_z(): return lax.ppermute(value, 'tp', [(s, (s + steps) % n) for s in range(n)])]
    unnamed x3 -> x0, blocking collectives: 97.5 us -> none
    ppermute x8 -> x62, starting transfers between devices: 17.6 us -> 77 us  [the longest x16 35.5 us: along_z(): return lax.ppermute(value, 'tp', [(s, (s + steps) % n) for s in range(n)])]
    select_n x0 -> x30, other arithmetic: none -> 31.2 us  [the longest x11 18.7 us: by_core(): return (jnp.where(self.is0, own, other), jnp.where(self.is0, other, own))]
  transfers between devices with their start and end apart: 21 -> 62, of which waited for: 13 -> 23; matrix products, arithmetic and copies ran while one was open for 23% -> 23% of each run, Pallas kernels for 0% -> 29%
where the time goes in v1:
time: 520 us; the launch traced here: 511 us
  waiting for transfers between devices  154 us (30%)
  Pallas kernels  149 us (29%)
  other arithmetic  82.6 us (16%)
  starting transfers between devices  77 us (15%)
  local copies, waits for them, and re-layouts  45.3 us (9%)
    ppermute x16, waiting for transfers between devices, along_z(): return lax.ppermute(value, 'tp', [(s, (s + steps) % n) for s in range(n)])  68.7 us
    ppermute x12, waiting for transfers between devices, along_a(): lax.ppermute(value, 'fsdp', self.pair_of(lambda a, b, c: ((a + steps) % A...  61.4 us
    pallas_call x1, Pallas kernels, attention(): pl.pallas_call(kernel, out_shape=(jax.ShapeDtypeStruct((T, H), bf16), jax...  37.4 us
    ppermute x16, starting transfers between devices, along_z(): return lax.ppermute(value, 'tp', [(s, (s + steps) % n) for s in range(n)])  35.5 us
    pallas_call x4, Pallas kernels, block_grads(): pl.pallas_call(kernel, out_shape=tuple((jax.ShapeDtypeStruct((len(chosen)...  27.7 us
    select_n x11, other arithmetic, by_core(): return (jnp.where(self.is0, own, other), jnp.where(self.is0, other, own))  18.7 us
    pallas_call x1, Pallas kernels, normed_grads(): pl.pallas_call(kernel, out_shape=(jax.ShapeDtypeStruct((T, D), bf16), jax...  16.8 us
    pallas_call x2, Pallas kernels, attn_weight_grads(): pl.pallas_call(kernel, out_shape=tuple((jax.ShapeDtypeStruct((len(chosen)...  16.6 us
  transfers between devices with their start and end apart: 62, of which 23 were waited for; matrix products, arithmetic and copies ran while one was open for 23% of the time, Pallas kernels for 29%

profile of v1, /device:TPU:0, one launch (start us, length us, event | category | flops | bytes accessed | tf_op | source)
XLA Modules:
  0.0 511.0 jit_solution(7723940396707200580)
XLA Ops:
  18.9 4.5 convert_reduce_fusion
  56.5 9.6 %collective-permute-start.1 = (bf16[128,2048]{1,0:T(8,128)(2,1)S(1)}, bf16[128,2048]{1,0:T(8,128)(2,1)S(1)}, u32[]{:S(2)}, u32[]{:S(2)}) collective-permute-start(bf16[128,2048]{1,0:T(8,128)(2,1)S(1)} %copy-done), channel_id=1, source_target_pairs={{0,1},{1,2},{2,3},{3,0},{4,5},{5,6},{6,7},{7,4},{8,9},{9,10},{10,1... | collective-permute-start | bytes 1572872 | tf_op jit(solution)/shard_map/ppermute | solution.py:85
  69.1 9.0 %collective-permute-done.1 = bf16[128,2048]{1,0:T(8,128)(2,1)S(1)} collective-permute-done((bf16[128,2048]{1,0:T(8,128)(2,1)S(1)}, bf16[128,2048]{1,0:T(8,128)(2,1)S(1)}, u32[]{:S(2)}, u32[]{:S(2)}) %collective-permute-start.1) | collective-permute-done | bytes 524320 | tf_op jit(solution)/shard_map/ppermute | solution.py:85
  91.2 5.0 collective-permute-done.3
  116.3 8.5 %collective-permute-done.13 = bf16[1024,256]{1,0:T(8,128)(2,1)S(1)} collective-permute-done((bf16[1024,256]{1,0:T(8,128)(2,1)S(1)}, bf16[1024,256]{1,0:T(8,128)(2,1)S(1)}, u32[]{:S(2)}, u32[]{:S(2)}) %collective-permute-start.13) | collective-permute-done | bytes 524320 | tf_op jit(solution)/shard_map/ppermute | solution.py:73
  128.1 8.0 %collective-permute-done.24 = bf16[256,1024]{1,0:T(8,128)(2,1)S(1)} collective-permute-done((bf16[256,1024]{1,0:T(8,128)(2,1)S(1)}, bf16[256,1024]{1,0:T(8,128)(2,1)S(1)}, u32[]{:S(2)}, u32[]{:S(2)}) %collective-permute-start.24) | collective-permute-done | bytes 524320 | tf_op jit(solution)/shard_map/ppermute | solution.py:73
  143.0 15.5 %collective-permute-done.12.p1.a1 = bf16[2,1024,256]{2,1,0:T(8,128)(2,1)S(1)} collective-permute-done((bf16[2,1024,256]{2,1,0:T(8,128)(2,1)S(1)}, bf16[2,1024,256]{2,1,0:T(8,128)(2,1)S(1)}, u32[]{:S(2)}, u32[]{:S(2)}) %collective-permute-start.12) | collective-permute-done | bytes 1048608 | tf_op jit(solution)/shard_map/ppermute | solution.py:73
  162.0 13.0 %project.1 = (bf16[1024,2048]{1,0:T(8,128)(2,1)}, bf16[1024,256]{1,0:T(8,128)(2,1)}, bf16[2,1024,256]{2,1,0:T(8,128)(2,1)}) custom-call(s32[8]{0:T(128)} %stack.101.offs, bf16[1024,2048]{1,0:T(8,128)(2,1)} %pad_maximum_fusion.rows_ref, f32[1,2048]{1,0:T(1,128)} %reshape.167.gain_ref, f32[1,2048]{1,0:T(1,128)} %reshape.168.shift_ref, ...), custom_call_target="tpu_custom_call" | custom-call | flops 3221225472 | bytes 14680064 | tf_op jit(solution)/shard_map/project/pallas_call | solution.py:261
  175.1 3.8 collective-permute-start.15
  182.7 11.7 %inner_forward.1 = (bf16[1024,1024]{1,0:T(8,128)(2,1)}, f32[1024,1024]{1,0:T(8,128)}) custom-call(s32[8]{0:T(128)} %stack.101.offs, bf16[1024,2048]{1,0:T(8,128)(2,1)} %get-tuple-element.42.x_ref.wide_ref, f32[1,1024]{1,0:T(1,128)} %bitcast.158, bf16[2,256,1024]{2,1,0:T(8,128)(2,1)} %pad_maximum_fusion.8.p0, ...), custom_call_target="tpu_custom_call" | custom-call | flops 4294967296 | bytes 14680064 | tf_op jit(solution)/shard_map/inner_forward/pallas_call | solution.py:453
  194.3 29.4 %collective-permute-done.28.p1 = bf16[2,1024,256]{2,1,0:T(8,128)(2,1)S(1)} collective-permute-done((bf16[2,1024,256]{2,1,0:T(8,128)(2,1)}, bf16[2,1024,256]{2,1,0:T(8,128)(2,1)S(1)}, u32[]{:S(2)}, u32[]{:S(2)}) %collective-permute-start.28) | collective-permute-done | bytes 1048608 | tf_op jit(solution)/shard_map/ppermute | solution.py:73
  224.7 10.1 %inner_backward.1 = (bf16[1024,1024]{1,0:T(8,128)(2,1)}, f32[1,1024]{1,0:T(1,128)}) custom-call(s32[8]{0:T(128)} %stack.101.offs, bf16[1024,2048]{1,0:T(8,128)(2,1)} %pad_maximum_fusion.1.cot_ref.c_ref.wide_ref, f32[1024,1024]{1,0:T(8,128)} %get-tuple-element.44.slope_ref, bf16[2,1024,256]{2,1,0:T(8,128)(2,1)} %pad_maximum_fusion.10.p0, ...), custom_call_target="tpu_custom_call" | custom-call | flops 4294967296 | bytes 14680064 | tf_op jit(solution)/shard_map/inner_backward/pallas_call | solution.py:490
  236.6 6.9 %inner_grads_far.1 = (bf16[2,256,1024]{2,1,0:T(8,128)(2,1)}, bf16[2,256,1024]{2,1,0:T(8,128)(2,1)}) custom-call(s32[8]{0:T(128)} %stack.101.offs, bf16[1024,2048]{1,0:T(8,128)(2,1)} %get-tuple-element.42.x_ref.wide_ref, bf16[1024,1024]{1,0:T(8,128)(2,1)} %get-tuple-element.45.pre_ref.narrow_ref), custom_call_target="tpu_custom_call" | custom-call | flops 2147483648 | bytes 8388608 | tf_op jit(solution)/shard_map/inner_grads_far/pallas_call | solution.py:532
  245.9 6.9 %outer_grads_far.1 = (bf16[2,1024,256]{2,1,0:T(8,128)(2,1)}, bf16[2,1024,256]{2,1,0:T(8,128)(2,1)}) custom-call(s32[8]{0:T(128)} %stack.101.offs, bf16[1024,2048]{1,0:T(8,128)(2,1)} %pad_maximum_fusion.1.cot_ref.c_ref.wide_ref, bf16[1024,1024]{1,0:T(8,128)(2,1)} %get-tuple-element.43.act_ref.narrow_ref), custom_call_target="tpu_custom_call" | custom-call | flops 2147483648 | bytes 8388608 | tf_op jit(solution)/shard_map/outer_grads_far/pallas_call | solution.py:532
  254.8 6.9 %inner_grads_near.1 = (bf16[2,256,1024]{2,1,0:T(8,128)(2,1)}, bf16[2,256,1024]{2,1,0:T(8,128)(2,1)}) custom-call(s32[8]{0:T(128)} %stack.101.offs, bf16[1024,2048]{1,0:T(8,128)(2,1)} %get-tuple-element.42.x_ref.wide_ref, bf16[1024,1024]{1,0:T(8,128)(2,1)} %get-tuple-element.45.pre_ref.narrow_ref), custom_call_target="tpu_custom_call" | custom-call | flops 2147483648 | bytes 8388608 | tf_op jit(solution)/shard_map/inner_grads_near/pallas_call | solution.py:532
  261.7 7.0 %outer_grads_near.1 = (bf16[2,1024,256]{2,1,0:T(8,128)(2,1)}, bf16[2,1024,256]{2,1,0:T(8,128)(2,1)}) custom-call(s32[8]{0:T(128)} %stack.101.offs, bf16[1024,2048]{1,0:T(8,128)(2,1)} %pad_maximum_fusion.1.cot_ref.c_ref.wide_ref, bf16[1024,1024]{1,0:T(8,128)(2,1)} %get-tuple-element.43.act_ref.narrow_ref), custom_call_target="tpu_custom_call" | custom-call | flops 2147483648 | bytes 8388608 | tf_op jit(solution)/shard_map/outer_grads_near/pallas_call | solution.py:532
  270.0 37.4 %attention.1 = (bf16[1024,256]{1,0:T(8,128)(2,1)}, bf16[1024,256]{1,0:T(8,128)(2,1)}, bf16[2,1024,256]{2,1,0:T(8,128)(2,1)}, f32[2,1024,256]{2,1,0:T(8,128)}) custom-call(s32[8]{0:T(128)} %stack.101.offs, bf16[1024,256]{1,0:T(8,128)(2,1)} %get-tuple-element.39.q_ref, bf16[2,1024,256]{2,1,0:T(8,128)(2,1)} %get-tuple-element.40.own_ref, ...), custom_call_target="tpu_custom_call" | custom-call | flops 16106127360 | bytes 9437184 | tf_op jit(solution)/shard_map/attention/pallas_call | solution.py:389
  324.3 11.8 %output_rows.1 = bf16[1024,2048]{1,0:T(8,128)(2,1)} custom-call(s32[8]{0:T(128)} %stack.101.offs, bf16[1024,256]{1,0:T(8,128)(2,1)} %get-tuple-element.41.att_ref, bf16[1024,1024]{1,0:T(8,128)(2,1)} %get-tuple-element.43.act_ref.narrow_ref, bf16[2,1024,256]{2,1,0:T(8,128)(2,1)} %copy-done.30, bf16[2,1024,256]{2,1,0:T(8,128)(2,1)} %copy-done.58, ...), custom_call_target="tpu_custom_call" | custom-call | flops 5368709120 | bytes 12058624 | tf_op jit(solution)/shard_map/output_rows/pallas_call | solution.py:598
  336.1 3.8 broadcast_select_fusion.1
  339.9 7.0 %collective-permute-done.53 = bf16[256,1024]{1,0:T(8,128)(2,1)S(1)} collective-permute-done((bf16[256,1024]{1,0:T(8,128)(2,1)}, bf16[256,1024]{1,0:T(8,128)(2,1)S(1)}, u32[]{:S(2)}, u32[]{:S(2)}) %collective-permute-start.53) | collective-permute-done | bytes 524320 | tf_op jit(solution)/shard_map/ppermute | solution.py:79
  349.7 6.4 %collective-permute-done.58 = bf16[1024,256]{1,0:T(8,128)(2,1)} collective-permute-done((bf16[1024,256]{1,0:T(8,128)(2,1)}, bf16[1024,256]{1,0:T(8,128)(2,1)}, u32[]{:S(2)}, u32[]{:S(2)}) %collective-permute-start.58) | collective-permute-done | bytes 524320 | tf_op jit(solution)/shard_map/ppermute | solution.py:79
  358.5 4.3 key_value_grads.1
  363.7 8.1 %attn_grads_far.1 = (bf16[2,1024,256]{2,1,0:T(8,128)(2,1)}, bf16[2,1024,256]{2,1,0:T(8,128)(2,1)}) custom-call(s32[8]{0:T(128)} %stack.101.offs, bf16[1024,2048]{1,0:T(8,128)(2,1)} %get-tuple-element.42.x_ref.wide_ref, bf16[1024,2048]{1,0:T(8,128)(2,1)} %pad_maximum_fusion.1.cot_ref.c_ref.wide_ref, bf16[1024,256]{1,0:T(8,128)(2,1)} %get-tuple-element.46.dq_ref, ...), custom_call_target="tpu_custom_call" | custom-call | flops 2147483648 | bytes 12582912 | tf_op jit(solution)/shard_map/attn_grads_far/pallas_call | solution.py:567
  373.8 16.8 %normed_grads.1 = (bf16[1024,2048]{1,0:T(8,128)(2,1)}, f32[8,2048]{1,0:T(8,128)}) custom-call(s32[8]{0:T(128)} %stack.101.offs, bf16[1024,1024]{1,0:T(8,128)(2,1)} %get-tuple-element.45.pre_ref.narrow_ref, bf16[1024,256]{1,0:T(8,128)(2,1)} %get-tuple-element.46.dq_ref, bf16[2,1024,256]{2,1,0:T(8,128)(2,1)} %get-tuple-element.49.dkv_ref, ...), custom_call_target="tpu_custom_call" | custom-call | flops 7516192768 | bytes 19398656 | tf_op jit(solution)/shard_map/normed_grads/pallas_call | solution.py:650
  392.0 8.6 %attn_grads_near.1 = (bf16[2,1024,256]{2,1,0:T(8,128)(2,1)}, bf16[2,1024,256]{2,1,0:T(8,128)(2,1)}) custom-call(s32[8]{0:T(128)} %stack.101.offs, bf16[1024,2048]{1,0:T(8,128)(2,1)} %get-tuple-element.42.x_ref.wide_ref, bf16[1024,2048]{1,0:T(8,128)(2,1)} %pad_maximum_fusion.1.cot_ref.c_ref.wide_ref, bf16[1024,256]{1,0:T(8,128)(2,1)} %get-tuple-element.46.dq_ref, ...), custom_call_target="tpu_custom_call" | custom-call | flops 2147483648 | bytes 12582912 | tf_op jit(solution)/shard_map/attn_grads_near/pallas_call | solution.py:567
  402.2 3.6 broadcast_select_fusion.7
  427.4 3.8 collective-permute-start.40
  431.7 6.7 %collective-permute-done.38 = bf16[64,2048]{1,0:T(8,128)(2,1)S(1)} collective-permute-done((bf16[64,2048]{1,0:T(8,128)(2,1)S(1)}, bf16[64,2048]{1,0:T(8,128)(2,1)S(1)}, u32[]{:S(2)}, u32[]{:S(2)}) %collective-permute-start.38) | collective-permute-done | bytes 262176 | tf_op jit(solution)/shard_map/ppermute | solution.py:85
  438.4 3.6 collective-permute-done.40
  446.8 16.1 %collective-permute-done.41 = bf16[128,2048]{1,0:T(8,128)(2,1)S(1)} collective-permute-done((bf16[128,2048]{1,0:T(8,128)(2,1)S(1)}, bf16[128,2048]{1,0:T(8,128)(2,1)S(1)}, u32[]{:S(2)}, u32[]{:S(2)}) %collective-permute-start.41) | collective-permute-done | bytes 524320 | tf_op jit(solution)/shard_map/ppermute | solution.py:85
  462.9 14.8 %collective-permute-done.39 = bf16[128,2048]{1,0:T(8,128)(2,1)S(1)} collective-permute-done((bf16[128,2048]{1,0:T(8,128)(2,1)S(1)}, bf16[128,2048]{1,0:T(8,128)(2,1)S(1)}, u32[]{:S(2)}, u32[]{:S(2)}) %collective-permute-start.39) | collective-permute-done | bytes 524320 | tf_op jit(solution)/shard_map/ppermute | solution.py:85
  478.3 8.5 %collective-permute-done.33 = bf16[128,2048]{1,0:T(8,128)(2,1)S(1)} collective-permute-done((bf16[128,2048]{1,0:T(8,128)(2,1)S(1)}, bf16[128,2048]{1,0:T(8,128)(2,1)S(1)}, u32[]{:S(2)}, u32[]{:S(2)}) %collective-permute-start.33) | collective-permute-done | bytes 524320 | tf_op jit(solution)/shard_map/ppermute | solution.py:85
  (398 shorter events, 191.8 us)
Async XLA Ops:
  0.7 87.0 %collective-permute-start.17 = (bf16[128,2048]{1,0:T(8,128)(2,1)}, bf16[128,2048]{1,0:T(8,128)(2,1)}, u32[]{:S(2)}, u32[]{:S(2)}) collective-permute-start(bf16[128,2048]{1,0:T(8,128)(2,1)} %param.26), channel_id=1, source_target_pairs={{0,1},{1,2},{2,3},{3,0},{4,5},{5,6},{6,7},{7,4},{8,9},{9,10},{10,1... | collective-permute-start | bytes 1572872 | tf_op jit(solution)/shard_map/ppermute | solution.py:85
  3.8 80.2 %collective-permute-start.16 = (bf16[128,2048]{1,0:T(8,128)(2,1)}, bf16[128,2048]{1,0:T(8,128)(2,1)}, u32[]{:S(2)}, u32[]{:S(2)}) collective-permute-start(bf16[128,2048]{1,0:T(8,128)(2,1)} %param.26), channel_id=1, source_target_pairs={{0,3},{1,0},{2,1},{3,2},{4,7},{5,4},{6,5},{7,6},{8,11},{9,8},{10,9... | collective-permute-start | bytes 1572872 | tf_op jit(solution)/shard_map/ppermute | solution.py:85
  12.7 43.7 %collective-permute-start.26 = (bf16[1024,256]{1,0:T(8,128)(2,1)}, bf16[1024,256]{1,0:T(8,128)(2,1)}, u32[]{:S(2)}, u32[]{:S(2)}) collective-permute-start(bf16[1024,256]{1,0:T(8,128)(2,1)} %broadcast_select_fusion.18), channel_id=1, source_target_pairs={{0,4},{4,0},{8,12},{12,8},{16,20},{20,16},{24,28},{28,24},{1,5},{5... | collective-permute-start | bytes 1572872 | tf_op jit(solution)/shard_map/ppermute | solution.py:69
  12.7 66.8 %collective-permute-start = (bf16[128,2048]{1,0:T(8,128)(2,1)}, bf16[128,2048]{1,0:T(8,128)(2,1)}, u32[]{:S(2)}, u32[]{:S(2)}) collective-permute-start(bf16[128,2048]{1,0:T(8,128)(2,1)} %param.15), channel_id=1, source_target_pairs={{0,3},{1,0},{2,1},{3,2},{4,7},{5,4},{6,5},{7,6},{8,11},{9,8},{10,9... | collective-permute-start | bytes 1572872 | tf_op jit(solution)/shard_map/ppermute | solution.py:85
  67.3 42.8 %collective-permute-start.21 = (bf16[256,1024]{1,0:T(8,128)(2,1)}, bf16[256,1024]{1,0:T(8,128)(2,1)S(1)}, u32[]{:S(2)}, u32[]{:S(2)}) collective-permute-start(bf16[256,1024]{1,0:T(8,128)(2,1)} %broadcast_select_fusion.10), channel_id=1, source_target_pairs={{0,4},{4,0},{8,12},{12,8},{16,20},{20,16},{24,28},{28,24},{1,5},{5... | collective-permute-start | bytes 1572872 | tf_op jit(solution)/shard_map/ppermute | solution.py:69
  78.0 32.6 %collective-permute-start.29 = (bf16[1024,256]{1,0:T(8,128)(2,1)S(1)}, bf16[1024,256]{1,0:T(8,128)(2,1)S(1)}, u32[]{:S(2)}, u32[]{:S(2)}) collective-permute-start(bf16[1024,256]{1,0:T(8,128)(2,1)S(1)} %get-tuple-element.92), channel_id=1, source_target_pairs={{0,16},{4,20},{8,24},{12,28},{16,0},{20,4},{24,8},{28,12},{1,17},{... | collective-permute-start | bytes 1572872 | tf_op jit(solution)/shard_map/ppermute | solution.py:73
  110.6 64.4 %collective-permute-start.20 = (bf16[512,2048]{1,0:T(8,128)(2,1)}, bf16[512,2048]{1,0:T(8,128)(2,1)S(1)}, u32[]{:S(2)}, u32[]{:S(2)}) collective-permute-start(bf16[512,2048]{1,0:T(8,128)(2,1)} %constant_dynamic-slice_fusion), channel_id=1, source_target_pairs={{0,4},{4,0},{8,12},{12,8},{16,20},{20,16},{24,28},{28,24},{1,5},{5... | collective-permute-start | bytes 6291464 | tf_op jit(solution)/shard_map/ppermute | solution.py:69
  124.8 33.7 %collective-permute-start.12 = (bf16[2,1024,256]{2,1,0:T(8,128)(2,1)S(1)}, bf16[2,1024,256]{2,1,0:T(8,128)(2,1)S(1)}, u32[]{:S(2)}, u32[]{:S(2)}) collective-permute-start(bf16[2,1024,256]{2,1,0:T(8,128)(2,1)S(1)} %pad_maximum_fusion.6.p0.a0), channel_id=1, source_target_pairs={{0,16},{4,20},{8,24},{12,28},{16,0},{20,4},{24,8},{28,12},{1,17},{... | collective-permute-start | bytes 3145736 | tf_op jit(solution)/shard_map/ppermute | solution.py:73
  125.5 33.6 %collective-permute-start.14 = (bf16[2,1024,256]{2,1,0:T(8,128)(2,1)S(1)}, bf16[2,1024,256]{2,1,0:T(8,128)(2,1)S(1)}, u32[]{:S(2)}, u32[]{:S(2)}) collective-permute-start(bf16[2,1024,256]{2,1,0:T(8,128)(2,1)S(1)} %pad_maximum_fusion.7.q0.b0), channel_id=1, source_target_pairs={{0,8},{4,12},{8,0},{12,4},{16,24},{20,28},{24,16},{28,20},{1,9},{5... | collective-permute-start | bytes 3145736 | tf_op jit(solution)/shard_map/ppermute | solution.py:79
  136.1 46.6 %collective-permute-start.23 = (bf16[2,256,1024]{2,1,0:T(8,128)(2,1)}, bf16[2,256,1024]{2,1,0:T(8,128)(2,1)}, u32[]{:S(2)}, u32[]{:S(2)}) collective-permute-start(bf16[2,256,1024]{2,1,0:T(8,128)(2,1)} %pad_maximum_fusion.8.p0), channel_id=1, source_target_pairs={{0,16},{4,20},{8,24},{12,28},{16,0},{20,4},{24,8},{28,12},{1,17},{... | collective-permute-start | bytes 3145736 | tf_op jit(solution)/shard_map/ppermute | solution.py:73
  137.6 45.0 %collective-permute-start.25 = (bf16[2,256,1024]{2,1,0:T(8,128)(2,1)}, bf16[2,256,1024]{2,1,0:T(8,128)(2,1)}, u32[]{:S(2)}, u32[]{:S(2)}) collective-permute-start(bf16[2,256,1024]{2,1,0:T(8,128)(2,1)} %pad_maximum_fusion.9.q0), channel_id=1, source_target_pairs={{0,8},{4,12},{8,0},{12,4},{16,24},{20,28},{24,16},{28,20},{1,9},{5... | collective-permute-start | bytes 3145736 | tf_op jit(solution)/shard_map/ppermute | solution.py:79
  158.5 65.2 %collective-permute-start.28 = (bf16[2,1024,256]{2,1,0:T(8,128)(2,1)}, bf16[2,1024,256]{2,1,0:T(8,128)(2,1)S(1)}, u32[]{:S(2)}, u32[]{:S(2)}) collective-permute-start(bf16[2,1024,256]{2,1,0:T(8,128)(2,1)} %pad_maximum_fusion.10.p0), channel_id=1, source_target_pairs={{0,16},{4,20},{8,24},{12,28},{16,0},{20,4},{24,8},{28,12},{1,17},{... | collective-permute-start | bytes 3145736 | tf_op jit(solution)/shard_map/ppermute | solution.py:73
  160.5 63.2 %collective-permute-start.30 = (bf16[2,1024,256]{2,1,0:T(8,128)(2,1)}, bf16[2,1024,256]{2,1,0:T(8,128)(2,1)}, u32[]{:S(2)}, u32[]{:S(2)}) collective-permute-start(bf16[2,1024,256]{2,1,0:T(8,128)(2,1)} %pad_maximum_fusion.11.q0), channel_id=1, source_target_pairs={{0,8},{4,12},{8,0},{12,4},{16,24},{20,28},{24,16},{28,20},{1,9},{5... | collective-permute-start | bytes 3145736 | tf_op jit(solution)/shard_map/ppermute | solution.py:79
  175.1 93.7 %collective-permute-start.15 = (bf16[2,1024,256]{2,1,0:T(8,128)(2,1)}, bf16[2,1024,256]{2,1,0:T(8,128)(2,1)}, u32[]{:S(2)}, u32[]{:S(2)}) collective-permute-start(bf16[2,1024,256]{2,1,0:T(8,128)(2,1)} %get-tuple-element.40.own_ref), channel_id=1, source_target_pairs={{0,8},{4,12},{8,16},{12,20},{16,24},{20,28},{1,9},{5,13},{9,17},{1... | collective-permute-start | bytes 3145736 | tf_op jit(solution)/shard_map/ppermute | solution.py:811
  243.5 65.3 %collective-permute-start.52 = (bf16[2,256,1024]{2,1,0:T(8,128)(2,1)}, bf16[2,256,1024]{2,1,0:T(8,128)(2,1)S(1)}, u32[]{:S(2)}, u32[]{:S(2)}) collective-permute-start(bf16[2,256,1024]{2,1,0:T(8,128)(2,1)} %get-tuple-element.59), channel_id=1, source_target_pairs={{0,16},{4,20},{8,24},{12,28},{16,0},{20,4},{24,8},{28,12},{1,17},{... | collective-permute-start | bytes 3145736 | tf_op jit(solution)/shard_map/ppermute | solution.py:73
  245.9 66.8 %collective-permute-start.54 = (bf16[2,256,1024]{2,1,0:T(8,128)(2,1)}, bf16[2,256,1024]{2,1,0:T(8,128)(2,1)S(1)}, u32[]{:S(2)}, u32[]{:S(2)}) collective-permute-start(bf16[2,256,1024]{2,1,0:T(8,128)(2,1)} %get-tuple-element.61), channel_id=1, source_target_pairs={{0,8},{4,12},{8,0},{12,4},{16,24},{20,28},{24,16},{28,20},{1,9},{5... | collective-permute-start | bytes 3145736 | tf_op jit(solution)/shard_map/ppermute | solution.py:79
  252.8 64.3 %collective-permute-start.57 = (bf16[2,1024,256]{2,1,0:T(8,128)(2,1)}, bf16[2,1024,256]{2,1,0:T(8,128)(2,1)S(1)}, u32[]{:S(2)}, u32[]{:S(2)}) collective-permute-start(bf16[2,1024,256]{2,1,0:T(8,128)(2,1)} %get-tuple-element.63), channel_id=1, source_target_pairs={{0,16},{4,20},{8,24},{12,28},{16,0},{20,4},{24,8},{28,12},{1,17},{... | collective-permute-start | bytes 3145736 | tf_op jit(solution)/shard_map/ppermute | solution.py:73
  252.8 67.9 %collective-permute-start.59 = (bf16[2,1024,256]{2,1,0:T(8,128)(2,1)}, bf16[2,1024,256]{2,1,0:T(8,128)(2,1)}, u32[]{:S(2)}, u32[]{:S(2)}) collective-permute-start(bf16[2,1024,256]{2,1,0:T(8,128)(2,1)} %get-tuple-element.65), channel_id=1, source_target_pairs={{0,8},{4,12},{8,0},{12,4},{16,24},{20,28},{24,16},{28,20},{1,9},{5... | collective-permute-start | bytes 3145736 | tf_op jit(solution)/shard_map/ppermute | solution.py:79
  307.5 51.0 %collective-permute-start.36 = (bf16[2,1024,256]{2,1,0:T(8,128)(2,1)}, bf16[2,1024,256]{2,1,0:T(8,128)(2,1)}, u32[]{:S(2)}, u32[]{:S(2)}) collective-permute-start(bf16[2,1024,256]{2,1,0:T(8,128)(2,1)} %get-tuple-element.48), channel_id=1, source_target_pairs={{8,0},{12,4},{16,8},{20,12},{24,16},{28,20},{9,1},{13,5},{17,9},{2... | collective-permute-start | bytes 3145736 | tf_op jit(solution)/shard_map/ppermute | solution.py:815
  310.1 36.8 %collective-permute-start.53 = (bf16[256,1024]{1,0:T(8,128)(2,1)}, bf16[256,1024]{1,0:T(8,128)(2,1)S(1)}, u32[]{:S(2)}, u32[]{:S(2)}) collective-permute-start(bf16[256,1024]{1,0:T(8,128)(2,1)} %fusion.32), channel_id=1, source_target_pairs={{0,8},{4,12},{8,0},{12,4},{16,24},{20,28},{24,16},{28,20},{1,9},{5... | collective-permute-start | bytes 1572872 | tf_op jit(solution)/shard_map/ppermute | solution.py:79
  314.1 32.8 %collective-permute-start.55 = (bf16[256,1024]{1,0:T(8,128)(2,1)}, bf16[256,1024]{1,0:T(8,128)(2,1)}, u32[]{:S(2)}, u32[]{:S(2)}) collective-permute-start(bf16[256,1024]{1,0:T(8,128)(2,1)} %fusion.33), channel_id=1, source_target_pairs={{0,16},{4,20},{8,24},{12,28},{16,0},{20,4},{24,8},{28,12},{1,17},{... | collective-permute-start | bytes 1572872 | tf_op jit(solution)/shard_map/ppermute | solution.py:73
  320.6 35.4 %collective-permute-start.58 = (bf16[1024,256]{1,0:T(8,128)(2,1)}, bf16[1024,256]{1,0:T(8,128)(2,1)}, u32[]{:S(2)}, u32[]{:S(2)}) collective-permute-start(bf16[1024,256]{1,0:T(8,128)(2,1)} %fusion.34), channel_id=1, source_target_pairs={{0,8},{4,12},{8,0},{12,4},{16,24},{20,28},{24,16},{28,20},{1,9},{5... | collective-permute-start | bytes 1572872 | tf_op jit(solution)/shard_map/ppermute | solution.py:79
  324.3 31.8 %collective-permute-start.60 = (bf16[1024,256]{1,0:T(8,128)(2,1)}, bf16[1024,256]{1,0:T(8,128)(2,1)}, u32[]{:S(2)}, u32[]{:S(2)}) collective-permute-start(bf16[1024,256]{1,0:T(8,128)(2,1)} %fusion.35), channel_id=1, source_target_pairs={{0,16},{4,20},{8,24},{12,28},{16,0},{20,4},{24,8},{28,12},{1,17},{... | collective-permute-start | bytes 1572872 | tf_op jit(solution)/shard_map/ppermute | solution.py:73
  346.9 62.3 %collective-permute-start.31 = (bf16[512,2048]{1,0:T(8,128)(2,1)}, bf16[512,2048]{1,0:T(8,128)(2,1)}, u32[]{:S(2)}, u32[]{:S(2)}) collective-permute-start(bf16[512,2048]{1,0:T(8,128)(2,1)} %broadcast_select_fusion.1), channel_id=1, source_target_pairs={{0,4},{4,0},{8,12},{12,8},{16,20},{20,16},{24,28},{28,24},{1,5},{5... | collective-permute-start | bytes 6291464 | tf_op jit(solution)/shard_map/ppermute | solution.py:69
  349.4 51.4 %collective-permute-start.56 = (f32[256,1024]{1,0:T(8,128)}, f32[256,1024]{1,0:T(8,128)}, u32[]{:S(2)}, u32[]{:S(2)}) collective-permute-start(f32[256,1024]{1,0:T(8,128)} %fusion.26), channel_id=1, source_target_pairs={{0,4},{4,0},{8,12},{12,8},{16,20},{20,16},{24,28},{28,24},{1,5},{5... | collective-permute-start | bytes 3145736 | tf_op jit(solution)/shard_map/ppermute | solution.py:69
  358.5 47.3 %collective-permute-start.61 = (f32[1024,256]{1,0:T(8,128)}, f32[1024,256]{1,0:T(8,128)}, u32[]{:S(2)}, u32[]{:S(2)}) collective-permute-start(f32[1024,256]{1,0:T(8,128)} %fusion.28), channel_id=1, source_target_pairs={{0,4},{4,0},{8,12},{12,8},{16,20},{20,16},{24,28},{28,24},{1,5},{5... | collective-permute-start | bytes 3145736 | tf_op jit(solution)/shard_map/ppermute | solution.py:69
  371.8 46.6 %collective-permute-start.47 = (bf16[2,1024,256]{2,1,0:T(8,128)(2,1)}, bf16[2,1024,256]{2,1,0:T(8,128)(2,1)}, u32[]{:S(2)}, u32[]{:S(2)}) collective-permute-start(bf16[2,1024,256]{2,1,0:T(8,128)(2,1)} %get-tuple-element.55), channel_id=1, source_target_pairs={{0,16},{4,20},{8,24},{12,28},{16,0},{20,4},{24,8},{28,12},{1,17},{... | collective-permute-start | bytes 3145736 | tf_op jit(solution)/shard_map/ppermute | solution.py:73
  373.5 48.3 %collective-permute-start.49 = (bf16[2,1024,256]{2,1,0:T(8,128)(2,1)}, bf16[2,1024,256]{2,1,0:T(8,128)(2,1)}, u32[]{:S(2)}, u32[]{:S(2)}) collective-permute-start(bf16[2,1024,256]{2,1,0:T(8,128)(2,1)} %get-tuple-element.57), channel_id=1, source_target_pairs={{0,8},{4,12},{8,0},{12,4},{16,24},{20,28},{24,16},{28,20},{1,9},{5... | collective-permute-start | bytes 3145736 | tf_op jit(solution)/shard_map/ppermute | solution.py:79
  431.4 46.9 %collective-permute-start.35 = (bf16[128,2048]{1,0:T(8,128)(2,1)S(1)}, bf16[128,2048]{1,0:T(8,128)(2,1)S(1)}, u32[]{:S(2)}, u32[]{:S(2)}) collective-permute-start(bf16[128,2048]{1,0:T(8,128)(2,1)S(1)} %pad_maximum_fusion.15), channel_id=1, source_target_pairs={{0,3},{1,0},{2,1},{3,2},{4,7},{5,4},{6,5},{7,6},{8,11},{9,8},{10,9... | collective-permute-start | bytes 1572872 | tf_op jit(solution)/shard_map/ppermute | solution.py:85
  444.3 33.4 %collective-permute-start.39 = (bf16[128,2048]{1,0:T(8,128)(2,1)S(1)}, bf16[128,2048]{1,0:T(8,128)(2,1)S(1)}, u32[]{:S(2)}, u32[]{:S(2)}) collective-permute-start(bf16[128,2048]{1,0:T(8,128)(2,1)S(1)} %pad_maximum_fusion.16), channel_id=1, source_target_pairs={{0,1},{1,2},{2,3},{3,0},{4,5},{5,6},{6,7},{7,4},{8,9},{9,10},{10,1... | collective-permute-start | bytes 1572872 | tf_op jit(solution)/shard_map/ppermute | solution.py:85
  444.5 42.4 %collective-permute-start.33 = (bf16[128,2048]{1,0:T(8,128)(2,1)S(1)}, bf16[128,2048]{1,0:T(8,128)(2,1)S(1)}, u32[]{:S(2)}, u32[]{:S(2)}) collective-permute-start(bf16[128,2048]{1,0:T(8,128)(2,1)S(1)} %pad_maximum_fusion.14), channel_id=1, source_target_pairs={{0,1},{1,2},{2,3},{3,0},{4,5},{5,6},{6,7},{7,4},{8,9},{9,10},{10,1... | collective-permute-start | bytes 1572872 | tf_op jit(solution)/shard_map/ppermute | solution.py:85
  446.8 51.2 %collective-permute-start.51 = (f32[1024,256]{1,0:T(8,128)}, f32[1024,256]{1,0:T(8,128)}, u32[]{:S(2)}, u32[]{:S(2)}) collective-permute-start(f32[1024,256]{1,0:T(8,128)} %fusion.24), channel_id=1, source_target_pairs={{0,4},{4,0},{8,12},{12,8},{16,20},{20,16},{24,28},{28,24},{1,5},{5... | collective-permute-start | bytes 3145736 | tf_op jit(solution)/shard_map/ppermute | solution.py:69
  (91 other events, 984.1 us)
